TPU v7x, 128 devices: a whole 4x4x4 slice. The times are simulated.
128 devices in a mesh: ctx: 16 (over x_hi, z, core), ch: 8 (over x_lo, y).
Axes of the slice: x: 4 (x_hi: 2, x_lo: 2; x = x_hi * 2 + x_lo), y: 4, z: 4, core: 2. Of those that a mesh axis runs over, the one named last changes fastest.
Arguments:
- features: bfloat16 [8192, 3, 4096], P('ctx', None, 'ch'), may hold values from -6 to 6
- residual_in: bfloat16 [8192, 4096], P('ctx', 'ch'), may hold values from -6 to 6
- short_filter: float32 [3, 7, 256], P(None, None, 'ch'), may hold values from -2 to 2
- medium_filter: float32 [128, 256], P(None, 'ch'), may hold values from -0.5 to 0.5
- skip_gain: float32 [4096], P('ch'), may hold values from -4 to 4
- out_weight: bfloat16 [4096, 4096], P('ch'), may hold values from -0.125 to 0.125
- norm_gain: float32 [4096], replicated, may hold values from 0.1 to 1.9
- attn_weight: bfloat16 [4096, 12288], P(None, 'ch'), may hold values from -2 to 2, as said below
- attn_out: bfloat16 [4096, 4096], P('ch'), may hold values from -0.125 to 0.125
Outputs:
- result: bfloat16 [8192, 4096], P('ctx', 'ch')
Inputs may be any that keep to these rules, and one draw needn't show every extreme that they name: `attn_weight`: entries of order 4096 ** -0.5 times a few.
All inputs are finite; a program needn't handle non-finite values.
Results may differ from a plain program's by a relative error of at most 0.03.
Values may be sent and summed in bfloat16 or wider, within the bound.
A program may use at most 128 MiB of HBM per device.

v0:
```python
import jax
import jax.numpy as jnp
from jax import lax
from jax.sharding import PartitionSpec as P

HEAD = 128
GROUP_SIZE = 16


norm_eps = 1e-05


def shifted(value, axis, steps):
    count = lax.axis_size(axis)
    initial, last = (max(0, -steps), min(count, count - steps))
    return lax.ppermute(value, axis, [(source, source + steps) for source in range(initial, last)])


def rotate_rows(block, positions):
    half_size = block.shape[-1] // 2
    frequency = 10000.0 ** (-jnp.arange(half_size, dtype=jnp.float32) * 2.0 / block.shape[-1])
    angles = positions.astype(jnp.float32)[:, None] * frequency[None, :]
    cosine = jnp.cos(angles)[:, None, :]
    sine_part = jnp.sin(angles)[:, None, :]
    first_half = block[..., :half_size]
    second_half = block[..., half_size:]
    return jnp.concatenate(
        [
            first_half * cosine - second_half * sine_part,
            second_half * cosine + first_half * sine_part,
        ],
        axis=-1,
    )


def featurize(extended, short_taps, row_count):
    lead_rows = short_taps.shape[1] - 1
    widened = extended.astype(jnp.float32)
    featured = jnp.zeros((row_count,) + extended.shape[1:], jnp.float32)
    for tap_index in range(short_taps.shape[1]):
        begin_row = lead_rows - tap_index
        featured = (
            featured
            + short_taps[:, tap_index, :][None] * widened[begin_row : begin_row + row_count]
        )
    return featured


def medium_mix(product_rim, product, filter_taps, skip_part):
    filter_len = filter_taps.shape[0]
    row_count, chan_count = product.shape
    group_count = filter_taps.shape[1]
    padded = jnp.concatenate(
        [jnp.zeros((1, chan_count), product.dtype), product_rim, product], axis=0
    )
    blocked = padded.reshape(
        row_count // filter_len + 1, filter_len, group_count, chan_count // group_count
    )
    windows = jnp.concatenate([blocked[:-1], blocked[1:]], axis=1).astype(jnp.float32)
    offsets = filter_len + jnp.arange(filter_len)[:, None] - jnp.arange(2 * filter_len)[None, :]
    inside = (offsets >= 0) & (offsets < filter_len)
    table = jnp.where(inside[:, :, None], filter_taps[jnp.clip(offsets, 0, filter_len - 1)], 0.0)
    toeplitz = jnp.transpose(table, (2, 0, 1))
    mixed = jnp.einsum("grs,nsgc->nrgc", toeplitz, windows, precision=lax.Precision.HIGHEST)
    return mixed.reshape(row_count, chan_count) + skip_part[None, :] * product.astype(jnp.float32)


def run_attention(queries, query_pos, key_rows, value_rows, position_of):
    head_count = queries.shape[1]
    row_count = queries.shape[0]
    head_size = queries.shape[2]
    scale_factor = 1.0 / head_size**0.5
    last_query = jnp.max(query_pos)
    initial = (
        jnp.zeros((head_count, row_count, head_size), jnp.float32),
        jnp.full((head_count, row_count), -1e30, jnp.float32),
        jnp.zeros((head_count, row_count), jnp.float32),
    )
    piece_keys = lax.all_gather(key_rows, "ctx", axis=0, tiled=True)
    piece_values = lax.all_gather(value_rows, "ctx", axis=0, tiled=True)
    piece_rows = piece_keys.shape[0]
    block_rows = 512

    def one_block(state_in, block_index):
        first_block = block_index * block_rows
        key_block = lax.dynamic_slice_in_dim(piece_keys, first_block, block_rows, 0)
        value_block = lax.dynamic_slice_in_dim(piece_values, first_block, block_rows, 0)
        key_pos = position_of(first_block + jnp.arange(block_rows))

        def update(state_old):
            acc_sum, run_max, run_total = state_old
            scores = (
                jnp.einsum("thd,khd->htk", queries, key_block, preferred_element_type=jnp.float32)
                * scale_factor
            )
            causal = (key_pos[None, :] <= query_pos[:, None])[None]
            block_max = jnp.max(jnp.where(causal, scores, -1e30), axis=-1)
            new_max = jnp.maximum(run_max, block_max)
            weights = jnp.where(causal, jnp.exp(scores - new_max[..., None]), 0.0)
            correction = jnp.exp(run_max - new_max)
            new_total = run_total * correction + jnp.sum(weights, axis=-1)
            update_sum = jnp.einsum(
                "htk,khd->htd",
                weights.astype(jnp.bfloat16),
                value_block,
                preferred_element_type=jnp.float32,
            )
            return (acc_sum * correction[..., None] + update_sum, new_max, new_total)

        def unchanged(state_old):
            return state_old

        state_out = lax.cond(jnp.min(key_pos) > last_query, unchanged, update, state_in)
        return (state_out, None)

    state_end, unused = lax.scan(one_block, initial, jnp.arange(piece_rows // block_rows))
    acc_sum, run_max, run_total = state_end
    output = acc_sum / run_total[..., None]
    return jnp.transpose(output, (1, 0, 2)).astype(jnp.bfloat16)


def shards(
    features,
    residual_in,
    short_filter,
    medium_filter,
    skip_gain,
    out_weight,
    norm_gain,
    attn_weight,
    attn_out,
):
    tok_rows = features.shape[0]
    chan_count = features.shape[2]
    short_taps = jnp.repeat(short_filter, GROUP_SIZE, axis=2)
    filter_len = medium_filter.shape[0]
    lead_rows = short_filter.shape[1] - 1
    rim_rows = shifted(features[tok_rows - lead_rows :], "ctx", 1)
    featured = featurize(jnp.concatenate([rim_rows, features], axis=0), short_taps, tok_rows)
    product = (featured[:, 1, :] * featured[:, 2, :]).astype(jnp.bfloat16)
    product_rim = shifted(product[tok_rows - (filter_len - 1) :], "ctx", 1)
    query_feat = featured[:, 0, :]
    mixed = medium_mix(product_rim, product, medium_filter, skip_gain)
    gated = (query_feat * mixed).astype(jnp.bfloat16)
    hyena_terms = jnp.dot(gated, out_weight, preferred_element_type=jnp.float32)
    hyena_out = lax.psum_scatter(
        hyena_terms.astype(jnp.bfloat16), "ch", scatter_dimension=1, tiled=True
    ).astype(jnp.float32)
    stream = (residual_in.astype(jnp.float32) + hyena_out).astype(jnp.bfloat16)
    stream_wide = stream.astype(jnp.float32)
    full_width = chan_count * lax.axis_size("ch")
    head_cols = attn_weight.shape[1]
    square_total = lax.psum(jnp.sum(stream_wide * stream_wide, axis=1), "ch")
    inverse = lax.rsqrt(square_total / full_width + norm_eps)
    gain_part = lax.dynamic_slice_in_dim(norm_gain, lax.axis_index("ch") * chan_count, chan_count)
    normed = (stream_wide * inverse[:, None] * gain_part[None, :]).astype(jnp.bfloat16)
    projected = jnp.dot(
        lax.all_gather(normed, "ch", axis=1, tiled=True),
        attn_weight,
        preferred_element_type=jnp.float32,
    )
    head_count = head_cols // (3 * HEAD)
    projected = projected.reshape(tok_rows, head_count, 3, HEAD)
    ctx_index = lax.axis_index("ctx")
    positions = ctx_index * tok_rows + jnp.arange(tok_rows, dtype=jnp.int32)
    queries = rotate_rows(projected[:, :, 0, :], positions).astype(jnp.bfloat16)
    key_rows = rotate_rows(projected[:, :, 1, :], positions).astype(jnp.bfloat16)
    value_rows = projected[:, :, 2, :].astype(jnp.bfloat16)

    def position_of(global_row):
        return global_row

    attended = run_attention(queries, positions, key_rows, value_rows, position_of)
    head_terms = jnp.dot(
        attended.reshape(tok_rows, head_count * HEAD), attn_out, preferred_element_type=jnp.float32
    )
    attn_mix = lax.psum_scatter(
        head_terms.astype(jnp.bfloat16), "ch", scatter_dimension=1, tiled=True
    ).astype(jnp.float32)
    return (stream_wide + attn_mix).astype(jnp.bfloat16)


def solution(mesh):
    in_specs = (
        P("ctx", None, "ch"),
        P("ctx", "ch"),
        P(None, None, "ch"),
        P(None, "ch"),
        P("ch"),
        P("ch", None),
        P(),
        P(None, "ch"),
        P("ch", None),
    )
    out_specs = P("ctx", "ch")
    return jax.shard_map(shards, mesh=mesh, in_specs=in_specs, out_specs=out_specs, check_vma=False)
```

profile of v0, /device:TPU:4, one launch (start us, length us, event | category | flops | bytes accessed | tf_op | source)
XLA Modules:
  0.0 683.3 jit_solution(12358582703660029944)
XLA Ops:
  12.8 109.0 %gather_fusion = f32[32768,32]{1,0:T(8,128)} fusion(f32[128,32]{1,0:T(8,128)S(1)} %copy.22, s32[32768]{0:T(1024)S(1)} %broadcast_clamp_fusion), kind=kCustom, calls=%fused_computation | custom fusion | bytes 8519680 | tf_op jit(solution)/shard_map/gather | solution.py:62
  121.8 11.7 %copy.23 = f32[128,256,32]{1,0,2:T(8,128)} copy(f32[128,256,32]{2,1,0:T(8,128)} %bitcast.98) | data formatting | bytes 8388608 | tf_op jit(solution)/shard_map/gather | solution.py:62
  134.4 7.0 %fusion.27 = f32[512,3,512]{0,2,1:T(8,128)S(1)} fusion(f32[518,3,512]{0,2,1:T(8,128)S(1)} %maximum_convert_fusion, f32[3,512]{1,0:T(4,128)S(1)} %get-tuple-element.252, f32[3,512]{1,0:T(4,128)S(1)} %get-tuple-element.253, f32[3,512]{1,0:T(4,128)S(1)} %get-tuple-element.254, f32[3,512]{1,0:T(4,128)S(1)} %get-tuple-element.255, ...), kind=kLoop, calls=%fused_computation.34 | loop fusion | flops 10223616 | bytes 25208832 | tf_op jit(solution)/shard_map/add | solution.py:43
  142.6 3.9 collective-permute-start.1
  147.4 2.0 convert_element_type.80
  152.5 2.0 pad_maximum_fusion
  157.6 5.2 fusion.35
  163.2 4.6 convolution_convert_fusion.1
  168.8 52.9 %reduce-scatter.3.cloned.1.call-done = bf16[512,512]{1,0:T(8,128)(2,1)} async-done(((bf16[512,4096]{1,0:T(8,128)(2,1)}), bf16[512,512]{1,0:T(8,128)(2,1)}) %reduce-scatter.3.cloned.1.call-update) | async-done | bytes 524304 | tf_op jit(solution)/shard_map/reduce_scatter | solution.py:146
  222.9 17.2 %psum.7 = f32[512]{0:T(512)S(1)} all-reduce(f32[512]{0:T(512)S(1)} %fusion.38), channel_id=1, replica_groups=mesh['ctx'=16,'ch'=8] {'ch'}, use_global_device_ids=true, to_apply=%region_2.3 | all-reduce | flops 512 | bytes 4096 | tf_op jit(solution)/shard_map/psum | solution.py:153
  240.2 2.0 fusion.40
  242.5 51.2 %all-gather.5.cloned.1.call-done = bf16[512,4096]{1,0:T(8,128)(2,1)} async-done(((bf16[512,512]{1,0:T(8,128)(2,1)}), bf16[512,4096]{1,0:T(8,128)(2,1)}) %all-gather.5.cloned.1.call-update) | async-done | bytes 4194320 | tf_op jit(solution)/shard_map/all_gather | solution.py:158
  293.7 10.6 %fusion.60 = f32[512,1536]{0,1:T(8,128)S(1)} fusion(bf16[512,4096]{1,0:T(8,128)(2,1)} %all-gather.5.cloned.1.call-done, bf16[4096,1536]{1,0:T(8,128)(2,1)} %param.20), kind=kOutput, calls=%fused_computation.107 | convolution fusion | flops 6442450944 | bytes 19922944 | tf_op jit(solution)/shard_map/dot_general | solution.py:157
  311.5 69.4 %all-gather.9.cloned.1.call-done = bf16[8192,4,1,128]{0,3,2,1:T(8,128)(2,1)} async-done(((bf16[512,4,1,128]{0,3,2,1:T(8,128)(2,1)}), bf16[8192,4,1,128]{0,3,2,1:T(8,128)(2,1)}) %all-gather.9.cloned.1.call-update) | async-done | bytes 8388624 | tf_op jit(solution)/shard_map/all_gather | solution.py:80
  380.9 12.0 %copy.29 = bf16[8192,4,128]{2,0,1:T(8,128)(2,1)} copy(bf16[8192,4,128]{0,2,1:T(8,128)(2,1)} %bitcast.99) | data formatting | bytes 16777216
  392.9 64.9 %all-gather.7.cloned.1.call-done = bf16[8192,4,128]{0,2,1:T(8,128)(2,1)} async-done(((bf16[512,4,128]{0,2,1:T(8,128)(2,1)}), bf16[8192,4,128]{0,2,1:T(8,128)(2,1)}) %all-gather.7.cloned.1.call-update) | async-done | bytes 8388624 | tf_op jit(solution)/shard_map/all_gather | solution.py:79
  457.8 12.0 %copy.27 = bf16[8192,4,128]{2,0,1:T(8,128)(2,1)} copy(bf16[8192,4,128]{0,2,1:T(8,128)(2,1)} %all-gather.7.cloned.1.call-done) | data formatting | bytes 16777216
  469.8 103.5 %while.15 = (s32[]{:T(128)}, f32[4,512,128]{2,1,0:T(8,128)S(1)}, f32[4,512]{1,0:T(4,128)S(1)}, f32[4,512]{1,0:T(4,128)S(1)}, s32[16]{0:T(128)S(1)}, /*index=5*/s...) while((s32[]{:T(128)}, f32[4,512,128]{2,1,0:T(8,128)S(1)}, ...), condition=%wide.region_10.11_spmd.clone, body=%wide.region_4.10_spmd.clone.sunk | while | flops 549197312 | bytes 17445200 | solution.py:116
  472.9 6.0 conditional.3
  473.1 2.0 fusion.2
  476.1 2.8 fusion.13
  482.0 6.0 conditional.3
  482.2 2.0 fusion.2
  485.2 2.8 fusion.13
  491.1 6.0 conditional.3
  491.3 2.0 fusion.2
  494.3 2.8 fusion.13
  500.2 6.0 conditional.3
  500.4 2.0 fusion.2
  503.4 2.8 fusion.13
  509.3 6.0 conditional.3
  509.5 2.0 fusion.2
  512.5 2.8 fusion.13
  518.4 6.0 conditional.3
  518.6 2.0 fusion.2
  521.6 2.8 fusion.13
  527.5 6.0 conditional.3
  527.7 2.0 fusion.2
  530.7 2.8 fusion.13
  536.5 6.0 conditional.3
  536.8 2.0 fusion.2
  539.8 2.8 fusion.13
  545.6 6.0 conditional.3
  545.9 2.0 fusion.2
  548.9 2.8 fusion.13
  573.8 6.5 convolution_convert_fusion
  580.3 94.4 %reduce-scatter.5.cloned.1.call-done = bf16[512,512]{1,0:T(8,128)(2,1)} async-done(((bf16[512,4096]{1,0:T(8,128)(2,1)}), bf16[512,512]{1,0:T(8,128)(2,1)}) %reduce-scatter.5.cloned.1.call-update) | async-done | bytes 524304 | tf_op jit(solution)/shard_map/reduce_scatter | solution.py:177
  674.7 2.0 fusion.41
  (200 shorter events, 55.3 us)
Async XLA Ops:
  6.5 6.2 copy-start.7
  6.5 215.1 %reduce-scatter.3.cloned.1.call-start = ((), (), s32[]{:S(2)}) async-start(), calls=%async_computation.2 | async-start | bytes 4718592 | tf_op jit(solution)/shard_map/reduce_scatter | solution.py:146
  7.6 126.0 %collective-permute-start = (bf16[6,3,512]{0,2,1:T(8,128)(2,1)S(1)}, bf16[6,3,512]{0,2,1:T(8,128)(2,1)S(1)}, u32[]{:S(2)}, u32[]{:S(2)}) collective-permute-start(bf16[6,3,512]{0,2,1:T(8,128)(2,1)S(1)} %copy.18), channel_id=1, source_target_pairs={{0,8},{8,16},{16,24},{24,32},{32,40},{40,48},{48,56},{56,64},{64,7... | collective-permute-start | bytes 55304 | tf_op jit(solution)/shard_map/ppermute | solution.py:16
  12.7 109.1 %copy-start.8 = (bf16[640]{0:T(1024)(128)(2,1)}, bf16[640]{0:T(1024)(128)(2,1)S(1)}, u32[]{:S(2)}) copy-start(bf16[640]{0:T(1024)(128)(2,1)S(1)} %pad.6.clone) | copy-start | bytes 3844
  141.5 11.0 %slice-start = ((bf16[640]{0:T(1024)(128)(2,1)}), bf16[512]{0:T(512)(128)(2,1)S(1)}, s32[]{:S(2)}) async-start(bf16[640]{0:T(1024)(128)(2,1)} %copy-done.8), calls=%async_computation.7 | async-start | bytes 2048 | tf_op jit(solution)/shard_map/slice | solution.py:59
  141.7 0.8 copy-start
  142.6 9.9 %collective-permute-start.1 = (bf16[127,512]{0,1:T(8,128)(2,1)S(1)}, bf16[127,512]{0,1:T(8,128)(2,1)S(1)}, u32[]{:S(2)}, u32[]{:S(2)}) collective-permute-start(bf16[127,512]{0,1:T(8,128)(2,1)S(1)} %slice_bitcast_fusion.3), channel_id=1, source_target_pairs={{0,8},{8,16},{16,24},{24,32},{32,40},{40,48},{48,56},{56,64},{64,7... | collective-permute-start | bytes 390152 | tf_op jit(solution)/shard_map/ppermute | solution.py:16
  157.6 5.6 copy-start.1
  157.6 5.6 copy-start.4
  157.6 5.6 copy-start.6
  167.9 53.8 %copy-start.2 = (bf16[512,512]{1,0:T(8,128)(2,1)S(1)}, bf16[512,512]{1,0:T(8,128)(2,1)}, u32[]{:S(2)}) copy-start(bf16[512,512]{1,0:T(8,128)(2,1)} %param.14) | copy-start | bytes 1572868
  167.9 125.8 %all-gather.5.cloned.1.call-start = ((), (), s32[]{:S(2)}) async-start(), calls=%async_computation.3 | async-start | bytes 4718592 | tf_op jit(solution)/shard_map/all_gather | solution.py:158
  242.3 138.7 %all-gather.9.cloned.1.call-start = ((), (), s32[]{:S(2)}) async-start(), calls=%async_computation.6 | async-start | bytes 8912896 | tf_op jit(solution)/shard_map/all_gather | solution.py:80
  304.3 1.6 copy-start.5
  306.9 150.9 %all-gather.7.cloned.1.call-start = ((), (), s32[]{:S(2)}) async-start(), calls=%async_computation.4 | async-start | bytes 8912896 | tf_op jit(solution)/shard_map/all_gather | solution.py:79
  310.5 364.2 %reduce-scatter.5.cloned.1.call-start = ((), (), s32[]{:S(2)}) async-start(), calls=%async_computation.5 | async-start | bytes 4718592 | tf_op jit(solution)/shard_map/reduce_scatter | solution.py:177
  580.3 94.4 %copy-start.3 = (bf16[512,512]{1,0:T(8,128)(2,1)S(1)}, bf16[512,512]{1,0:T(8,128)(2,1)}, u32[]{:S(2)}) copy-start(bf16[512,512]{1,0:T(8,128)(2,1)} %reduce-scatter.3.cloned.1.call-done) | copy-start | bytes 1572868
Sparse Core Ops, SparseCore 0:
  168.0 53.5 reduce-scatter.2
  242.4 51.2 all-gather.4
  307.0 73.8 all-gather.8
  383.1 74.6 all-gather.6
  580.5 94.2 reduce-scatter.4
where the time goes:
time: 688 us; the launch traced here: 683 us
  waiting for transfers between devices  334 us (49%)
  local copies, waits for them, and re-layouts  172 us (25%)
  matrix products  70.4 us (10%)
  other arithmetic  39.1 us (6%)
  loops' own time  30.6 us (4%)
  blocking collectives  17.2 us (2%)
  between operations  13.5 us (2%)
    gather x2, local copies, waits for them, and re-layouts, medium_mix(): filter_taps[jnp.clip(offsets, 0, filter_len - 1)]  121 us
    reduce_scatter x1, waiting for transfers between devices, shards(): lax.psum_scatter(head_terms.astype(jnp.bfloat16), 'ch', scatter_dimension...  94.4 us
    all_gather x1, waiting for transfers between devices, run_attention(): piece_values = lax.all_gather(value_rows, 'ctx', axis=0, tiled=True)  69.4 us
    all_gather x1, waiting for transfers between devices, run_attention(): piece_keys = lax.all_gather(key_rows, 'ctx', axis=0, tiled=True)  64.9 us
    reduce_scatter x1, waiting for transfers between devices, shards(): lax.psum_scatter(hyena_terms.astype(jnp.bfloat16), 'ch', scatter_dimensio...  52.9 us
    all_gather x1, waiting for transfers between devices, shards(): lax.all_gather(normed, 'ch', axis=1, tiled=True)  51.2 us
    another operation x1, loops' own time, run_attention(): lax.scan(one_block, initial, jnp.arange(piece_rows // block_rows))  29.8 us
    unnamed x28, local copies, waits for them, and re-layouts  28.6 us
  transfers between devices with their start and end apart: 7, of which 6 were waited for; matrix products, arithmetic and copies ran while one was open for 21% of the time, Pallas kernels for 0%

commit v1 on v0

v1 whole, which is shorter than its diff:
```python
import functools

import jax
import jax.numpy as jnp
from jax import lax
from jax.experimental import pallas as pl
from jax.experimental.pallas import tpu as pltpu
from jax.sharding import PartitionSpec as P

HEAD = 128
GROUP_SIZE = 16
N_CH = 8
N_CTX = 16
N_Y = 4
N_Z = 4
HALO = 144

norm_eps = 1e-05
MESH = pl.DeviceIdType.MESH
VMEM_LIMIT = 60 * 1024 * 1024


def remote(src, dst, send_sem, recv_sem, target):
    return pltpu.make_async_remote_copy(
        src_ref=src, dst_ref=dst, send_sem=send_sem, recv_sem=recv_sem,
        device_id=target, device_id_type=MESH,
    )


def greet(targets):
    barrier = pltpu.get_barrier_semaphore()
    for target in targets:
        pl.semaphore_signal(barrier, inc=1, device_id=target, device_id_type=MESH)
    pl.semaphore_wait(barrier, len(targets))


def whole(count):
    return [pl.BlockSpec(memory_space=pltpu.VMEM)] * count


def hyena_kernel(feat_ref, short_ref, medium_ref, skip_ref, out_ref,
                 halo, ext, taps, product, product_t, query, mixed_t, send_sem, recv_sem):
    rows, chans = out_ref.shape
    ctx = lax.axis_index("ctx")
    chan = lax.axis_index("ch")
    after = (lax.rem(ctx + 1, N_CTX), chan)
    before = (lax.rem(ctx + N_CTX - 1, N_CTX), chan)
    greet([after, before])
    near = remote(feat_ref.at[pl.ds(0, 1), pl.ds(rows - 16, 16)], halo.at[pl.ds(0, 1), pl.ds(HALO - 16, 16)],
                  send_sem.at[0], recv_sem.at[0], after)
    far = remote(feat_ref.at[pl.ds(1, 2), pl.ds(rows - HALO, HALO)], halo.at[pl.ds(1, 2)],
                 send_sem.at[1], recv_sem.at[1], after)
    near.start()
    far.start()

    groups = short_ref.shape[2]
    spread = (lax.broadcasted_iota(jnp.int32, (groups, chans), 1) // GROUP_SIZE
              == lax.broadcasted_iota(jnp.int32, (groups, chans), 0)).astype(jnp.float32)
    for kind in range(3):
        taps[kind, 0:7, :] = jnp.dot(short_ref[kind], spread, preferred_element_type=jnp.float32,
                                     precision=lax.Precision.HIGHEST)
        ext[kind, HALO:, :] = feat_ref[kind].astype(jnp.float32)

    def featured(kind, first, count):
        slab = ext[kind, pl.ds(first - 8 if isinstance(first, int) else pl.multiple_of(first - 8, 8), count + 8), :]
        total = taps[kind, 0:1, :] * slab[8:]
        for tap in range(1, 7):
            total = total + taps[kind, tap : tap + 1, :] * pltpu.roll(slab, tap, 0)[8:]
        return total

    def main_rows(step, carry):
        first = pl.multiple_of(16 + step * 16, 16)
        query[pl.ds(first, 16), :] = featured(0, pl.multiple_of(first + HALO, 16), 16)
        product[pl.ds(first + 128, 16), :] = featured(1, pl.multiple_of(first + HALO, 16), 16) * featured(2, pl.multiple_of(first + HALO, 16), 16)
        return carry

    lax.fori_loop(0, rows // 16 - 1, main_rows, 0)
    near.wait()
    far.wait()
    keep = (ctx > 0).astype(jnp.float32)
    ext[0, HALO - 16 : HALO, :] = halo[0, HALO - 16 : HALO, :].astype(jnp.float32) * keep
    for kind in (1, 2):
        ext[kind, 0:HALO, :] = halo[kind].astype(jnp.float32) * keep
    query[0:16, :] = featured(0, HALO, 16)

    def rim_rows(step, carry):
        first = pl.multiple_of(step * 16, 16)
        product[pl.ds(first, 16), :] = featured(1, pl.multiple_of(first + 16, 16), 16) * featured(2, pl.multiple_of(first + 16, 16), 16)
        return carry

    lax.fori_loop(0, 9, rim_rows, 0)
    for block in range(5):
        product_t[:, 128 * block : 128 * block + 128] = (
            product[128 * block : 128 * block + 128, :].T.astype(jnp.bfloat16))
    row = lax.broadcasted_iota(jnp.int32, (128, 128), 0)
    col = lax.broadcasted_iota(jnp.int32, (128, 128), 1)

    def one_group(group, carry):
        line = jnp.broadcast_to(medium_ref[pl.ds(group, 1), :], (128, 128))
        wheel = pltpu.roll(line, 0, 1, stride=1, stride_axis=0)
        table = jnp.concatenate([jnp.where(col < row, wheel, 0.0), jnp.where(col >= row, wheel, 0.0)],
                                axis=0).astype(jnp.bfloat16)
        lane = pl.ds(pl.multiple_of(group * GROUP_SIZE, GROUP_SIZE), GROUP_SIZE)
        window = jnp.concatenate(
            [product_t[lane, 128 * block : 128 * block + 256] for block in range(4)], axis=0)
        mix = jnp.dot(window, table, preferred_element_type=jnp.float32)
        for block in range(4):
            mixed_t[lane, 128 * block : 128 * block + 128] = mix[16 * block : 16 * block + 16, :]
        return carry

    lax.fori_loop(0, groups, one_group, 0)
    for block in range(4):
        part = pl.ds(128 * block, 128)
        mix = mixed_t[:, part].T
        inner = product[pl.ds(128 * block + 128, 128), :].astype(jnp.bfloat16).astype(jnp.float32)
        out_ref[part, :] = (query[part, :] * (mix + skip_ref[...] * inner)).astype(jnp.bfloat16)


def hyena(feats, short_filter, medium_t, skip_row):
    kinds, rows, chans = feats.shape
    return pl.pallas_call(
        hyena_kernel,
        out_shape=jax.ShapeDtypeStruct((rows, chans), jnp.bfloat16),
        in_specs=whole(4),
        out_specs=pl.BlockSpec(memory_space=pltpu.VMEM),
        scratch_shapes=[
            pltpu.VMEM((3, HALO, chans), jnp.bfloat16),
            pltpu.VMEM((3, HALO + rows, chans), jnp.float32),
            pltpu.VMEM((3, 8, chans), jnp.float32),
            pltpu.VMEM((128 + rows, chans), jnp.float32),
            pltpu.VMEM((chans, 128 + rows), jnp.bfloat16),
            pltpu.VMEM((rows, chans), jnp.float32),
            pltpu.VMEM((chans, rows), jnp.float32),
            pltpu.SemaphoreType.DMA((2,)),
            pltpu.SemaphoreType.DMA((2,)),
        ],
        compiler_params=pltpu.CompilerParams(collective_id=0, has_side_effects=True, vmem_limit_bytes=VMEM_LIMIT),
        name="hyena",
    )(feats, short_filter, medium_t, skip_row)


def project_kernel(left_ref, base_ref, own_ref, other_ref, out_ref,
                   w_own, w_other, left_in, outbox, inbox, kept,
                   w_sem, x_send, x_recv, y_send, y_recv):
    rows, depth = left_ref.shape
    width = depth
    ctx = lax.axis_index("ctx")
    chan = lax.axis_index("ch")
    y_pos = lax.rem(chan, N_Y)
    x_lo = chan // N_Y
    partner = (ctx, (1 - x_lo) * N_Y + y_pos)
    column = [(ctx, x_lo * N_Y + lax.rem(y_pos + step, N_Y)) for step in range(1, N_Y)]
    half = pl.ds(pl.multiple_of(x_lo * (N_Y * width), N_Y * width), N_Y * width)
    load_own = pltpu.make_async_copy(own_ref.at[:, half], w_own, w_sem.at[0])
    load_other = pltpu.make_async_copy(other_ref, w_other, w_sem.at[1])
    load_own.start()
    load_other.start()
    greet([partner] + column)
    pieces = 4
    tall = rows // pieces
    crossing = []
    for piece in range(pieces):
        part = pl.ds(piece * tall, tall)
        copy = remote(left_ref.at[part], left_in.at[part], x_send.at[piece], x_recv.at[piece], partner)
        copy.start()
        crossing.append(copy)
    load_own.wait()
    load_other.wait()
    sent = []
    for piece in range(pieces):
        part = pl.ds(piece * tall, tall)
        crossing[piece].wait_recv()
        mine = left_ref[part, :]
        theirs = left_in[part, :]
        for step in (2, 1, 3, 0):
            target = lax.rem(y_pos + step, N_Y)
            cols = pl.ds(pl.multiple_of(target * width, width), width)
            term = (jnp.dot(mine, w_own[:, cols], preferred_element_type=jnp.float32)
                    + jnp.dot(theirs, w_other[:, cols], preferred_element_type=jnp.float32))
            if step == 0:
                kept[part, :] = term + base_ref[part, :].astype(jnp.float32)
            else:
                outbox[step - 1, part, :] = term.astype(jnp.bfloat16)
                copy = remote(outbox.at[step - 1, part], inbox.at[step - 1, part],
                              y_send.at[step - 1, piece], y_recv.at[step - 1, piece], column[step - 1])
                copy.start()
                sent.append(copy)
    for piece in range(pieces):
        part = pl.ds(piece * tall, tall)
        total = kept[part, :]
        for step in (2, 1, 3):
            sent[piece * 3 + (2, 1, 3).index(step)].wait_recv()
            total = total + inbox[step - 1, part, :].astype(jnp.float32)
        out_ref[part, :] = total.astype(jnp.bfloat16)
    for copy in crossing + sent:
        copy.wait_send()


def project(left, base, own_weight, other_half, collective_id):
    rows, depth = left.shape
    width = depth
    return pl.pallas_call(
        project_kernel,
        out_shape=jax.ShapeDtypeStruct((rows, width), jnp.bfloat16),
        in_specs=whole(2) + [pl.BlockSpec(memory_space=pl.ANY)] * 2,
        out_specs=pl.BlockSpec(memory_space=pltpu.VMEM),
        scratch_shapes=[
            pltpu.VMEM((depth, N_Y * width), jnp.bfloat16),
            pltpu.VMEM((depth, N_Y * width), jnp.bfloat16),
            pltpu.VMEM((rows, depth), jnp.bfloat16),
            pltpu.VMEM((3, rows, width), jnp.bfloat16),
            pltpu.VMEM((3, rows, width), jnp.bfloat16),
            pltpu.VMEM((rows, width), jnp.float32),
            pltpu.SemaphoreType.DMA((2,)),
            pltpu.SemaphoreType.DMA((4,)),
            pltpu.SemaphoreType.DMA((4,)),
            pltpu.SemaphoreType.DMA((3, 4)),
            pltpu.SemaphoreType.DMA((3, 4)),
        ],
        compiler_params=pltpu.CompilerParams(collective_id=collective_id, has_side_effects=True,
                                             vmem_limit_bytes=VMEM_LIMIT),
        name="project",
    )(left, base, own_weight, other_half)


def partner_half(weight):
    rows, cols = weight.shape
    chan = lax.axis_index("ch")
    ctx = lax.axis_index("ctx")
    x_lo = chan // N_Y
    piece = lax.dynamic_slice(weight, (ctx * (rows // N_CTX), (1 - x_lo) * (cols // 2)), (rows // N_CTX, cols // 2))
    piece = lax.ppermute(piece, "ch", [(source, (source + N_Y) % N_CH) for source in range(N_CH)])
    return lax.all_gather(piece, "ctx", axis=0, tiled=True)


def qkv_kernel(stream_ref, gain_ref, cos_ref, sin_ref, w_hbm, out_ref,
               blocks, w_ref, acc, squares, w_sem, send_sem, recv_sem):
    rows, width = stream_ref.shape
    ctx = lax.axis_index("ctx")
    chan = lax.axis_index("ch")
    y_pos = lax.rem(chan, N_Y)
    x_lo = chan // N_Y
    x_hi = 1 - x_lo
    up, down, opposite = lax.rem(y_pos + 1, N_Y), lax.rem(y_pos + 3, N_Y), lax.rem(y_pos + 2, N_Y)
    dev_up = (ctx, x_lo * N_Y + up)
    dev_down = (ctx, x_lo * N_Y + down)
    dev_x = (ctx, x_hi * N_Y + y_pos)
    load = pltpu.make_async_copy(w_hbm, w_ref, w_sem)
    load.start()
    greet([dev_up, dev_down, dev_x])
    tall = rows // 2
    halves = [pl.ds(0, tall), pl.ds(tall, tall)]

    def slot(x, y):
        return x * N_Y + y

    sent = {}

    def push(name, src, where, part, target):
        index = len(sent)
        copy = remote(src, blocks.at[where, part], send_sem.at[index], recv_sem.at[index], target)
        copy.start()
        sent[name] = copy

    mine = slot(x_lo, y_pos)
    for number, part in enumerate(halves):
        push(("x", number), stream_ref.at[part], mine, part, dev_x)
        push(("up", number), stream_ref.at[part], mine, part, dev_up)
        push(("down", number), stream_ref.at[part], mine, part, dev_down)

    load.wait()
    squares[...] = jnp.zeros_like(squares)

    def use(block, where, first):
        wide = block.astype(jnp.float32)
        square = wide * wide
        squares[...] += (square[:, 0:128] + square[:, 128:256]) + (square[:, 256:384] + square[:, 384:512])
        cols = pl.ds(pl.multiple_of(where * width, width), width)
        scaled = (wide * gain_ref[:, cols]).astype(jnp.bfloat16)
        term = jnp.dot(scaled, w_ref[cols, :], preferred_element_type=jnp.float32)
        acc[...] = term if first else acc[...] + term

    use(stream_ref[...], mine, True)
    sent["up", 0].wait_recv()
    push(("upup", 0), blocks.at[slot(x_lo, down), halves[0]], slot(x_lo, down), halves[0], dev_up)
    sent["down", 0].wait_recv()
    sent["down", 1].wait_recv()
    push(("downdown", 0), blocks.at[slot(x_lo, up), halves[1]], slot(x_lo, up), halves[1], dev_down)
    sent["x", 0].wait_recv()
    other = slot(x_hi, y_pos)
    push(("xup", 0), blocks.at[other, halves[0]], other, halves[0], dev_up)
    push(("xdown", 0), blocks.at[other, halves[0]], other, halves[0], dev_down)
    sent["x", 1].wait_recv()
    push(("xup", 1), blocks.at[other, halves[1]], other, halves[1], dev_up)
    push(("xdown", 1), blocks.at[other, halves[1]], other, halves[1], dev_down)
    use(blocks[slot(x_lo, up)], slot(x_lo, up), False)
    sent["upup", 0].wait_recv()
    far = slot(x_lo, opposite)
    push(("far", 0), blocks.at[far, halves[0]], far, halves[0], dev_x)
    sent["downdown", 0].wait_recv()
    push(("far", 1), blocks.at[far, halves[1]], far, halves[1], dev_x)
    sent["up", 1].wait_recv()
    use(blocks[slot(x_lo, down)], slot(x_lo, down), False)
    use(blocks[other], other, False)
    use(blocks[far], far, False)
    for name, y in (("xdown", up), ("xup", down), ("far", opposite)):
        sent[name, 0].wait_recv()
        sent[name, 1].wait_recv()
        use(blocks[slot(x_hi, y)], slot(x_hi, y), False)

    inverse = lax.rsqrt(jnp.sum(squares[...], axis=1, keepdims=True) / (N_CH * width) + norm_eps)
    scale = HEAD ** -0.5 * 1.4426950408889634
    for head in range(4):
        for kind in range(3):
            first = (head * 3 + kind) * HEAD
            value = acc[:, first : first + HEAD] * inverse
            if kind < 2:
                value = value * cos_ref[...] + pltpu.roll(value, HEAD // 2, 1) * sin_ref[...]
            if kind == 0:
                value = value * scale
            out_ref[head, kind] = value.astype(jnp.bfloat16)
    for copy in sent.values():
        copy.wait_send()


def gathered_qkv(stream, gain_row, cosine, sine, weight):
    rows, width = stream.shape
    heads = weight.shape[1] // (3 * HEAD)
    return pl.pallas_call(
        qkv_kernel,
        out_shape=jax.ShapeDtypeStruct((heads, 3, rows, HEAD), jnp.bfloat16),
        in_specs=whole(4) + [pl.BlockSpec(memory_space=pl.ANY)],
        out_specs=pl.BlockSpec(memory_space=pltpu.VMEM),
        scratch_shapes=[
            pltpu.VMEM((N_CH, rows, width), jnp.bfloat16),
            pltpu.VMEM(weight.shape, jnp.bfloat16),
            pltpu.VMEM((rows, weight.shape[1]), jnp.float32),
            pltpu.VMEM((rows, 128), jnp.float32),
            pltpu.SemaphoreType.DMA,
            pltpu.SemaphoreType.DMA((14,)),
            pltpu.SemaphoreType.DMA((14,)),
        ],
        compiler_params=pltpu.CompilerParams(collective_id=2, has_side_effects=True, vmem_limit_bytes=VMEM_LIMIT),
        name="gather_qkv",
    )(stream, gain_row, cosine, sine, weight)


def attention_kernel(qkv_ref, out_ref, queries, keyvals, acc, peak, outbox,
                     own_sem, q_send, q_recv, z_send, z_recv, s_send, s_recv,
                     h_send, h_recv, t_send, t_recv, o_send, o_recv):
    heads, kinds, rows, head = qkv_ref.shape
    ctx = lax.axis_index("ctx")
    chan = lax.axis_index("ch")
    core = lax.rem(ctx, 2)
    z_pos = lax.rem(ctx // 2, N_Z)
    high = ctx // (2 * N_Z)

    def place(x, z, c):
        return ((x * N_Z + z) * 2 + c, chan)

    sibling = place(high, z_pos, 1 - core)
    across = place(1 - high, z_pos, core)
    ring = [place(high, lax.rem(z_pos + step, N_Z), core) for step in range(1, N_Z)]
    greet(ring + [sibling, across])

    def source(step):
        return lax.rem(z_pos + N_Z - step, N_Z)

    own_q = pltpu.make_async_copy(qkv_ref.at[z_pos, 0], queries.at[z_pos], own_sem.at[0])
    own_kv = pltpu.make_async_copy(qkv_ref.at[z_pos, pl.ds(1, 2)], keyvals.at[high, z_pos, core], own_sem.at[1])
    own_kv.start()
    own_q.start()
    z_copies, q_copies = [], []
    for step in (1, 2, 3):
        target = lax.rem(z_pos + step, N_Z)
        copy = remote(qkv_ref.at[target, pl.ds(1, 2)], keyvals.at[high, z_pos, core],
                      z_send.at[step - 1], z_recv.at[step - 1], ring[step - 1])
        copy.start()
        z_copies.append(copy)
    for step in (1, 2, 3):
        target = lax.rem(z_pos + step, N_Z)
        copy = remote(qkv_ref.at[target, 0], queries.at[z_pos],
                      q_send.at[step - 1], q_recv.at[step - 1], ring[step - 1])
        copy.start()
        q_copies.append(copy)
    shares, hops = [], []

    def spread(step):
        place_here = keyvals.at[high, source(step), core]
        share = remote(place_here, place_here, s_send.at[step], s_recv.at[step], sibling)
        share.start()
        shares.append(share)
        hop = remote(place_here, place_here, h_send.at[step], h_recv.at[step], across)
        hops.append(hop)

        @pl.when(high == 0)
        def _():
            hop.start()

    own_kv.wait()
    spread(0)
    for step in (1, 3, 2):
        z_copies[step - 1].wait_recv()
        spread(step)
    own_q.wait()
    for copy in q_copies:
        copy.wait_recv()
    for share in shares:
        share.wait_recv()

    row = lax.broadcasted_iota(jnp.int32, (rows, rows), 0)
    col = lax.broadcasted_iota(jnp.int32, (rows, rows), 1)
    ones = jnp.ones((rows, head), jnp.bfloat16)

    def update(block, x, z, c, diagonal):
        scores = lax.dot_general(queries[block], keyvals[x, z, c, 0], (((1,), (1,)), ((), ())),
                                 preferred_element_type=jnp.float32)
        if diagonal:
            scores = jnp.where(col <= row, scores, -1e30)
        top = jnp.max(scores, axis=1, keepdims=True)
        if not diagonal:
            old = peak[block]
            new = jnp.maximum(old, top)
            peak[block] = new
            shrink = jnp.exp2(old - new)[:, 0:1]
        else:
            new = jnp.broadcast_to(top, (rows, head))
            peak[block] = new
        weights = jnp.exp2(scores - new[:, 0:1]).astype(jnp.bfloat16)
        wide = jnp.concatenate([keyvals[x, z, c, 1], ones], axis=1)
        term = jnp.dot(weights, wide, preferred_element_type=jnp.float32)
        acc[block] = term if diagonal else acc[block] * shrink + term

    def own_part(block, carry):
        update(block, high, block, core, True)

        def earlier(index, inner):
            update(block, high, index // 2, lax.rem(index, 2), False)
            return inner

        lax.fori_loop(0, 2 * block + core, earlier, 0)
        return carry

    lax.fori_loop(0, N_Z, own_part, 0)

    @pl.when(high == 1)
    def _():
        passes = []
        for order, step in enumerate((0, 1, 3, 2)):
            hops[order].wait_recv()
            landed = keyvals.at[0, source(step), core]
            copy = remote(landed, landed, t_send.at[step], t_recv.at[step], sibling)
            copy.start()
            passes.append(copy)
        for copy in passes:
            copy.wait_recv()

        def low_part(block, carry):
            def each(index, inner):
                update(block, 0, index // 2, lax.rem(index, 2), False)
                return inner

            lax.fori_loop(0, 2 * N_Z, each, 0)
            return carry

        lax.fori_loop(0, N_Z, low_part, 0)
        for copy in passes:
            copy.wait_send()

    backs = []
    for step in (2, 1, 3, 0):
        target = lax.rem(z_pos + step, N_Z)
        result = acc[target]
        outbox[target] = (result[:, :head] / result[:, head:]).astype(jnp.bfloat16)
        lanes = pl.ds(pl.multiple_of(z_pos * head, head), head)
        if step == 0:
            out_ref[:, lanes] = outbox[target]
        else:
            copy = remote(outbox.at[target], out_ref.at[:, lanes], o_send.at[step - 1], o_recv.at[step - 1],
                          ring[step - 1])
            copy.start()
            backs.append(copy)
    for copy in backs:
        copy.wait_recv()
    for copy in z_copies + q_copies + shares + backs:
        copy.wait_send()

    @pl.when(high == 0)
    def _():
        for hop in hops:
            hop.wait_send()


def attention(qkv):
    heads, kinds, rows, head = qkv.shape
    dma = pltpu.SemaphoreType.DMA
    return pl.pallas_call(
        attention_kernel,
        out_shape=jax.ShapeDtypeStruct((rows, heads * head), jnp.bfloat16),
        in_specs=whole(1),
        out_specs=pl.BlockSpec(memory_space=pltpu.VMEM),
        scratch_shapes=[
            pltpu.VMEM((N_Z, rows, head), jnp.bfloat16),
            pltpu.VMEM((2, N_Z, 2, 2, rows, head), jnp.bfloat16),
            pltpu.VMEM((N_Z, rows, 2 * head), jnp.float32),
            pltpu.VMEM((N_Z, rows, head), jnp.float32),
            pltpu.VMEM((N_Z, rows, head), jnp.bfloat16),
            dma((2,)), dma((3,)), dma((3,)), dma((3,)), dma((3,)), dma((4,)), dma((4,)),
            dma((4,)), dma((4,)), dma((4,)), dma((4,)), dma((3,)), dma((3,)),
        ],
        compiler_params=pltpu.CompilerParams(collective_id=3, has_side_effects=True, vmem_limit_bytes=VMEM_LIMIT),
        name="attention",
    )(qkv)


def rotation_tables(rows):
    positions = lax.axis_index("ctx") * rows + jnp.arange(rows, dtype=jnp.int32)
    half_size = HEAD // 2
    frequency = 10000.0 ** (-jnp.arange(half_size, dtype=jnp.float32) * 2.0 / HEAD)
    angles = positions.astype(jnp.float32)[:, None] * frequency[None, :]
    cosine, sine = jnp.cos(angles), jnp.sin(angles)
    return jnp.concatenate([cosine, cosine], axis=1), jnp.concatenate([-sine, sine], axis=1)


def shards(features, residual_in, short_filter, medium_filter, skip_gain, out_weight, norm_gain, attn_weight,
           attn_out):
    rows = features.shape[0]
    out_half = partner_half(out_weight)
    attn_half = partner_half(attn_out)
    cosine, sine = rotation_tables(rows)
    gated = hyena(jnp.transpose(features, (1, 0, 2)), short_filter, medium_filter.T, skip_gain[None, :])
    stream = project(gated, residual_in, out_weight, out_half, 1)
    qkv = gathered_qkv(stream, norm_gain[None, :], cosine, sine, attn_weight)
    attended = attention(qkv)
    return project(attended, stream, attn_out, attn_half, 4)


def solution(mesh):
    in_specs = (
        P("ctx", None, "ch"),
        P("ctx", "ch"),
        P(None, None, "ch"),
        P(None, "ch"),
        P("ch"),
        P("ch", None),
        P(),
        P(None, "ch"),
        P("ch", None),
    )
    out_specs = P("ctx", "ch")
    return jax.shard_map(shards, mesh=mesh, in_specs=in_specs, out_specs=out_specs, check_vma=False)
```

time: 688 us -> 265 us (0.39)
  waiting for transfers between devices: 334 us -> 25.8 us
  Pallas kernels: 0 us -> 216 us
  local copies, waits for them, and re-layouts: 172 us -> 5 us
  matrix products: 70.4 us -> 0 us
  other arithmetic: 39.1 us -> 2.01 us
  loops' own time: 30.6 us -> 0 us
  blocking collectives: 17.2 us -> 0 us
    pallas_call x0 -> x5, Pallas kernels: none -> 216 us  [the longest x1 91.2 us: attention(): pl.pallas_call(attention_kernel, out_shape=jax.ShapeDtypeStruct((rows, he...]
    all_gather x3 -> x2, waiting for transfers between devices: 185 us -> 17.9 us  [partner_half(): return lax.all_gather(piece, 'ctx', axis=0, tiled=True)]
    reduce_scatter x2 -> x0, waiting for transfers between devices: 147 us -> none  [the longest x1 94.4 us: shards(): lax.psum_scatter(head_terms.astype(jnp.bfloat16), 'ch', scatter_dimension...]
    gather x2 -> x0, local copies, waits for them, and re-layouts: 121 us -> none  [medium_mix(): filter_taps[jnp.clip(offsets, 0, filter_len - 1)]]
    dot_general x22 -> x0, matrix products: 70.4 us -> none  [the longest x9 25.3 us: update(): jnp.einsum('htk,khd->htd', weights.astype(jnp.bfloat16), value_block, pre...]
    another operation x17 -> x0, loops' own time: 30.6 us -> none  [the longest x1 29.8 us: run_attention(): lax.scan(one_block, initial, jnp.arange(piece_rows // block_rows))]
    unnamed x28 -> x5, local copies, waits for them, and re-layouts: 28.6 us -> 3.17 us
    psum x1 -> x0, blocking collectives: 17.2 us -> none  [shards(): square_total = lax.psum(jnp.sum(stream_wide * stream_wide, axis=1), 'ch')]
  transfers between devices with their start and end apart: 7 -> 4, of which waited for: 6 -> 3; matrix products, arithmetic and copies ran while one was open for 21% -> 1% of each run, Pallas kernels for 0% -> 70%
where the time goes in v1:
time: 265 us
  Pallas kernels  216 us (82%)
  waiting for transfers between devices  25.8 us (10%)
  between operations  13.5 us (5%)
  local copies, waits for them, and re-layouts  5 us (2%)
    pallas_call x1, Pallas kernels, attention(): pl.pallas_call(attention_kernel, out_shape=jax.ShapeDtypeStruct((rows, he...  91.2 us
    pallas_call x2, Pallas kernels, project(): pl.pallas_call(project_kernel, out_shape=jax.ShapeDtypeStruct((rows, widt...  66.4 us
    pallas_call x1, Pallas kernels, gathered_qkv(): pl.pallas_call(qkv_kernel, out_shape=jax.ShapeDtypeStruct((heads, 3, rows...  36.5 us
    pallas_call x1, Pallas kernels, hyena(): pl.pallas_call(hyena_kernel, out_shape=jax.ShapeDtypeStruct((rows, chans)...  21.7 us
    all_gather x2, waiting for transfers between devices, partner_half(): return lax.all_gather(piece, 'ctx', axis=0, tiled=True)  17.9 us
    ppermute x2, waiting for transfers between devices, partner_half(): lax.ppermute(piece, 'ch', [(source, (source + N_Y) % N_CH) for source in...  7.81 us
  transfers between devices with their start and end apart: 4, of which 3 were waited for; matrix products, arithmetic and copies ran while one was open for 1% of the time, Pallas kernels for 70%

profile of v1, /device:TPU:4, one launch (start us, length us, event | category | flops | bytes accessed | tf_op | source)
XLA Modules:
  0.0 264.7 jit_solution(18384312921046156990)
XLA Ops:
  6.5 0.0 all-gather.3.cloned.1.call-start
  6.5 0.9 dynamic_slice.6
  7.5 1.3 collective-permute-start
  8.7 4.0 %collective-permute-done = bf16[32,2048]{1,0:T(8,128)(2,1)S(1)} collective-permute-done((bf16[32,2048]{1,0:T(8,128)(2,1)S(1)}, bf16[32,2048]{1,0:T(8,128)(2,1)S(1)}, u32[]{:S(2)}, u32[]{:S(2)}) %collective-permute-start) | collective-permute-done | bytes 131104 | tf_op jit(solution)/shard_map/ppermute | solution.py:232
  12.8 0.0 copy-start
  12.8 0.6 copy-done
  13.4 0.0 all-gather.3.cloned.1.call-update
  13.4 0.0 all-gather.5.cloned.1.call-start
  13.5 0.9 dynamic_slice.7
  14.4 1.3 collective-permute-start.1
  15.7 3.8 %collective-permute-done.1 = bf16[32,2048]{1,0:T(8,128)(2,1)S(1)} collective-permute-done((bf16[32,2048]{1,0:T(8,128)(2,1)S(1)}, bf16[32,2048]{1,0:T(8,128)(2,1)S(1)}, u32[]{:S(2)}, u32[]{:S(2)}) %collective-permute-start.1) | collective-permute-done | bytes 131104 | tf_op jit(solution)/shard_map/ppermute | solution.py:232
  19.5 0.0 copy-start.1
  19.5 0.6 copy-done.1
  20.1 0.0 all-gather.5.cloned.1.call-update
  20.1 21.7 %hyena.1.left_ref = bf16[512,512]{1,0:T(8,128)(2,1)} custom-call(bf16[3,512,512]{2,1,0:T(8,128)(2,1)} %bitcast.4, f32[3,7,32]{2,1,0:T(8,128)} %short_ref.1, f32[32,128]{1,0:T(8,128)} %bitcast.5, f32[1,512]{1,0:T(1,128)} %bitcast.7), custom_call_target="tpu_custom_call" | custom-call | tf_op jit(solution)/shard_map/hyena/pallas_call | solution.py:121
  41.9 1.0 fusion
  42.9 1.0 pad_maximum_fusion
  43.9 17.9 %all-gather.3.cloned.1.call-done.other_ref = bf16[512,2048]{1,0:T(8,128)(2,1)} async-done(((bf16[32,2048]{1,0:T(8,128)(2,1)}), bf16[512,2048]{1,0:T(8,128)(2,1)}) %all-gather.3.cloned.1.call-update) | async-done | bytes 2097168 | tf_op jit(solution)/shard_map/all_gather | solution.py:233
  61.9 35.4 %project.2.stream_ref.base_ref = bf16[512,512]{1,0:T(8,128)(2,1)} custom-call(bf16[512,512]{1,0:T(8,128)(2,1)} %hyena.1.left_ref, bf16[512,512]{1,0:T(8,128)(2,1)} %base_ref.1, bf16[512,4096]{1,0:T(8,128)(2,1)} %own_ref.2, bf16[512,2048]{1,0:T(8,128)(2,1)} %all-gather.3.cloned.1.call-done.other_ref), custom_call_target="tpu_custom_call" | custom-call | tf_op jit(solution)/shard_map/project/pallas_call | solution.py:202
  97.2 36.5 %gather_qkv.1.qkv_ref = bf16[4,3,512,128]{3,2,1,0:T(8,128)(2,1)} custom-call(bf16[512,512]{1,0:T(8,128)(2,1)} %project.2.stream_ref.base_ref, f32[1,4096]{1,0:T(1,128)} %bitcast.6, f32[512,128]{1,0:T(8,128)} %get-tuple-element.8.cos_ref, f32[512,128]{1,0:T(8,128)} %get-tuple-element.9.sin_ref, bf16[4096,1536]{1,0:T(8,128)(2,1)} %w_hbm.1), custom_call_target="tpu_custom_call" | custom-call | tf_op jit(solution)/shard_map/gather_qkv/pallas_call | solution.py:329
  133.7 91.2 %attention.1.left_ref = bf16[512,512]{1,0:T(8,128)(2,1)} custom-call(bf16[4,3,512,128]{3,2,1,0:T(8,128)(2,1)} %gather_qkv.1.qkv_ref), custom_call_target="tpu_custom_call" | custom-call | tf_op jit(solution)/shard_map/attention/pallas_call | solution.py:497
  224.9 0.0 all-gather.5.cloned.1.call-done.other_ref
  225.0 31.0 %project.3 = bf16[512,512]{1,0:T(8,128)(2,1)} custom-call(bf16[512,512]{1,0:T(8,128)(2,1)} %attention.1.left_ref, bf16[512,512]{1,0:T(8,128)(2,1)} %project.2.stream_ref.base_ref, bf16[512,4096]{1,0:T(8,128)(2,1)} %own_ref.3, bf16[512,2048]{1,0:T(8,128)(2,1)} %all-gather.5.cloned.1.call-done.other_ref), custom_call_target="tpu_custom_call" | custom-call | tf_op jit(solution)/shard_map/project/pallas_call | solution.py:202
  255.9 1.9 copy.11
  (2 shorter events, 0.0 us)
Async XLA Ops:
  6.5 55.3 %all-gather.3.cloned.1.call-start = ((), (), s32[]{:S(2)}) async-start(), calls=%async_computation | async-start | bytes 2228224 | tf_op jit(solution)/shard_map/all_gather | solution.py:233
  7.5 5.3 %collective-permute-start = (bf16[32,2048]{1,0:T(8,128)(2,1)S(1)}, bf16[32,2048]{1,0:T(8,128)(2,1)S(1)}, u32[]{:S(2)}, u32[]{:S(2)}) collective-permute-start(bf16[32,2048]{1,0:T(8,128)(2,1)S(1)} %dynamic_slice.6), channel_id=1, source_target_pairs={{0,4},{1,5},{2,6},{3,7},{4,0},{5,1},{6,2},{7,3},{8,12},{9,13},{10,... | collective-permute-start | bytes 393224 | tf_op jit(solution)/shard_map/ppermute | solution.py:232
  12.8 0.7 copy-start
  13.4 211.5 %all-gather.5.cloned.1.call-start = ((), (), s32[]{:S(2)}) async-start(), calls=%async_computation.1 | async-start | bytes 2228224 | tf_op jit(solution)/shard_map/all_gather | solution.py:233
  14.4 5.0 %collective-permute-start.1 = (bf16[32,2048]{1,0:T(8,128)(2,1)S(1)}, bf16[32,2048]{1,0:T(8,128)(2,1)S(1)}, u32[]{:S(2)}, u32[]{:S(2)}) collective-permute-start(bf16[32,2048]{1,0:T(8,128)(2,1)S(1)} %dynamic_slice.7), channel_id=1, source_target_pairs={{0,4},{1,5},{2,6},{3,7},{4,0},{5,1},{6,2},{7,3},{8,12},{9,13},{10,... | collective-permute-start | bytes 393224 | tf_op jit(solution)/shard_map/ppermute | solution.py:232
  19.5 0.6 copy-start.1
Sparse Core Ops, SparseCore 0:
  13.6 48.2 all-gather.2
  64.3 48.7 all-gather.4

commit v2 on v1

--- a/solution.py
+++ b/solution.py
@@ -38,26 +38,222 @@
     return [pl.BlockSpec(memory_space=pltpu.VMEM)] * count
 
 
-def hyena_kernel(feat_ref, short_ref, medium_ref, skip_ref, out_ref,
-                 halo, ext, taps, product, product_t, query, mixed_t, send_sem, recv_sem):
+def ring_z():
+    ctx = lax.axis_index("ctx")
+    chan = lax.axis_index("ch")
+    core = lax.rem(ctx, 2)
+    z_pos = lax.rem(ctx // 2, N_Z)
+    base = ctx - z_pos * 2 - core
+    sibling = (base + z_pos * 2 + 1 - core, chan)
+    ring = [(base + lax.rem(z_pos + step, N_Z) * 2 + core, chan) for step in range(1, N_Z)]
+    return core, z_pos, sibling, ring
+
+
+def piece_rows(z_pos, core, tall):
+    return pl.ds(pl.multiple_of((z_pos * 2 + core) * tall, tall), tall)
+
+
+class Spread:
+    def __init__(self, piece_ref, whole_ref, send_sem, recv_sem):
+        self.piece, self.whole = piece_ref, whole_ref
+        self.send, self.recv = send_sem, recv_sem
+        self.core, self.z_pos, self.sibling, self.ring = ring_z()
+        self.tall = whole_ref.shape[0] // (2 * N_Z)
+        self.copies = []
+
+    def push(self, src, rows, target):
+        index = len(self.copies)
+        copy = remote(src, self.whole.at[rows], self.send.at[index], self.recv.at[index], target)
+        copy.start()
+        self.copies.append(copy)
+
+    def first(self):
+        rows = piece_rows(self.z_pos, self.core, self.tall)
+        for target in self.ring + [self.sibling]:
+            self.push(self.piece, rows, target)
+
+    def second(self):
+        for step in (1, 3, 2):
+            self.copies[step - 1].wait_recv()
+            rows = piece_rows(lax.rem(self.z_pos + N_Z - step, N_Z), self.core, self.tall)
+            self.push(self.whole.at[rows], rows, self.sibling)
+
+    def finish(self):
+        for copy in self.copies[3:]:
+            copy.wait_recv()
+        for copy in self.copies:
+            copy.wait_send()
+
+
+PIECES = 4
+
+
+def column_places():
+    ctx = lax.axis_index("ctx")
+    chan = lax.axis_index("ch")
+    y_pos = lax.rem(chan, N_Y)
+    x_lo = chan // N_Y
+    partner = (ctx, (1 - x_lo) * N_Y + y_pos)
+    up = (ctx, x_lo * N_Y + lax.rem(y_pos + 1, N_Y))
+    down = (ctx, x_lo * N_Y + lax.rem(y_pos + 3, N_Y))
+    return y_pos, x_lo, partner, up, down
+
+
+def piece_of(ref, piece):
+    tall = ref.shape[0] // PIECES
+    return ref.at[pl.ds(piece * tall, tall)]
+
+
+def cross(left, left_in, partner, x_send, x_recv, piece):
+    copy = remote(piece_of(left, piece), piece_of(left_in, piece), x_send.at[piece], x_recv.at[piece], partner)
+    copy.start()
+    return copy
+
+
+def scatter_sum(left, left_in, crossing, base, out, w_own, w_other, boxes, up, down, y_pos):
+    outbox, inbox, relay_out, relay_in, pending, kept, y_send, y_recv, r_send, r_recv = boxes
+    rows, width = left.shape
+    tall = rows // PIECES
+    ways = (up, down)
+    copies = []
+
+    def term(piece, step):
+        cols = pl.ds(pl.multiple_of(lax.rem(y_pos + step, N_Y) * width, width), width)
+        part = pl.ds(piece * tall, tall)
+        return (jnp.dot(left[part, :], w_own[:, cols], preferred_element_type=jnp.float32)
+                + jnp.dot(left_in[part, :], w_other[:, cols], preferred_element_type=jnp.float32))
+
+    def send(way, piece, value):
+        outbox[way, piece] = value.astype(jnp.bfloat16)
+        copy = remote(outbox.at[way, piece], inbox.at[way, piece], y_send.at[way, piece], y_recv.at[way, piece],
+                      ways[way])
+        copy.start()
+        copies.append(copy)
+        return copy
+
+    arrivals = {}
+    relays = []
+
+    def combine(piece):
+        relays[piece].wait_recv()
+        way = piece % 2
+        arrivals[way, piece] = send(way, piece, pending[piece] + relay_in[piece].astype(jnp.float32))
+
+    for piece in range(PIECES):
+        crossing[piece].wait_recv()
+        way = piece % 2
+        relay_out[piece] = term(piece, 2).astype(jnp.bfloat16)
+        relay = remote(relay_out.at[piece], relay_in.at[piece], r_send.at[piece], r_recv.at[piece], ways[way])
+        relay.start()
+        relays.append(relay)
+        arrivals[1 - way, piece] = send(1 - way, piece, term(piece, (1, 3)[1 - way]))
+        pending[piece] = term(piece, (1, 3)[way])
+        part = pl.ds(piece * tall, tall)
+        kept[part, :] = term(piece, 0) + base[part, :].astype(jnp.float32)
+        if piece:
+            combine(piece - 1)
+    combine(PIECES - 1)
+
+    def finish():
+        for piece in range(PIECES):
+            part = pl.ds(piece * tall, tall)
+            for way in (1 - piece % 2, piece % 2):
+                arrivals[way, piece].wait_recv()
+            total = kept[part, :] + inbox[0, piece].astype(jnp.float32) + inbox[1, piece].astype(jnp.float32)
+            out[part, :] = total.astype(jnp.bfloat16)
+        for copy in list(crossing) + copies + relays:
+            copy.wait_send()
+
+    return finish
+
+
+def box_shapes(rows, width):
+    tall = rows // PIECES
+    dma = pltpu.SemaphoreType.DMA
+    return [
+        pltpu.VMEM((2, PIECES, tall, width), jnp.bfloat16),
+        pltpu.VMEM((2, PIECES, tall, width), jnp.bfloat16),
+        pltpu.VMEM((PIECES, tall, width), jnp.bfloat16),
+        pltpu.VMEM((PIECES, tall, width), jnp.bfloat16),
+        pltpu.VMEM((PIECES, tall, width), jnp.float32),
+        pltpu.VMEM((rows, width), jnp.float32),
+        dma((2, PIECES)), dma((2, PIECES)), dma((PIECES,)), dma((PIECES,)),
+    ]
+
+
+def project_kernel(left_ref, base_ref, own_ref, other_ref, out_ref, w_own, w_other, left_in, w_sem, x_send, x_recv,
+                   *boxes):
+    y_pos, x_lo, partner, up, down = column_places()
+    span = w_own.shape[1]
+    half = pl.ds(pl.multiple_of(x_lo * span, span), span)
+    load_own = pltpu.make_async_copy(own_ref.at[:, half], w_own, w_sem.at[0])
+    load_other = pltpu.make_async_copy(other_ref, w_other, w_sem.at[1])
+    load_own.start()
+    load_other.start()
+    greet([partner, up, down])
+    crossing = [cross(left_ref, left_in, partner, x_send, x_recv, piece) for piece in range(PIECES)]
+    load_own.wait()
+    load_other.wait()
+    scatter_sum(left_ref, left_in, crossing, base_ref, out_ref, w_own, w_other, boxes, up, down, y_pos)()
+
+
+def project(left, base, own_weight, other_half):
+    rows, depth = left.shape
+    dma = pltpu.SemaphoreType.DMA
+    return pl.pallas_call(
+        project_kernel,
+        out_shape=jax.ShapeDtypeStruct((rows, depth), jnp.bfloat16),
+        in_specs=whole(2) + [pl.BlockSpec(memory_space=pl.ANY)] * 2,
+        out_specs=pl.BlockSpec(memory_space=pltpu.VMEM),
+        scratch_shapes=[
+            pltpu.VMEM((depth, N_Y * depth), jnp.bfloat16),
+            pltpu.VMEM((depth, N_Y * depth), jnp.bfloat16),
+            pltpu.VMEM((rows, depth), jnp.bfloat16),
+            dma((2,)), dma((PIECES,)), dma((PIECES,)),
+        ] + box_shapes(rows, depth),
+        compiler_params=pltpu.CompilerParams(collective_id=4, has_side_effects=True, vmem_limit_bytes=VMEM_LIMIT),
+        name="project",
+    )(left, base, own_weight, other_half)
+
+
+def hyena_kernel(feat_ref, short_ref, medium_ref, skip_ref, base_ref, first_weight, second_weight,
+                 out_ref, second_half,
+                 halo, ext, taps, product, product_t, query, mixed_t, send_sem, recv_sem,
+                 w_own, first_half, gated, gated_in, w_sem, x_send, x_recv, g_send, g_recv,
+                 w_send, w_recv, v_send, v_recv, *boxes):
     rows, chans = out_ref.shape
     ctx = lax.axis_index("ctx")
     chan = lax.axis_index("ch")
     after = (lax.rem(ctx + 1, N_CTX), chan)
     before = (lax.rem(ctx + N_CTX - 1, N_CTX), chan)
-    greet([after, before])
+    y_pos, x_lo, partner, up, down = column_places()
+    core, z_pos, sibling, ring = ring_z()
+    span = first_half.shape[1]
+    load_own = pltpu.make_async_copy(
+        first_weight.at[:, pl.ds(pl.multiple_of(x_lo * span, span), span)], w_own, w_sem)
+    load_own.start()
+    greet([after, before, partner, sibling, up, down] + ring)
     near = remote(feat_ref.at[pl.ds(0, 1), pl.ds(rows - 16, 16)], halo.at[pl.ds(0, 1), pl.ds(HALO - 16, 16)],
                   send_sem.at[0], recv_sem.at[0], after)
     far = remote(feat_ref.at[pl.ds(1, 2), pl.ds(rows - HALO, HALO)], halo.at[pl.ds(1, 2)],
                  send_sem.at[1], recv_sem.at[1], after)
     near.start()
     far.start()
+    tall = first_half.shape[0] // (2 * N_Z)
+    mine = piece_rows(z_pos, core, tall)
+    half = pl.ds(pl.multiple_of((1 - x_lo) * span, span), span)
+    cross_first = remote(first_weight.at[mine, half], first_half.at[mine], x_send.at[0], x_recv.at[0], partner)
+    cross_second = remote(second_weight.at[mine, half], second_half.at[mine], x_send.at[1], x_recv.at[1], partner)
+    cross_first.start()
+    cross_second.start()
+    spread = Spread(first_half.at[mine], first_half, w_send, w_recv)
+    later = Spread(second_half.at[mine], second_half, v_send, v_recv)
 
     groups = short_ref.shape[2]
-    spread = (lax.broadcasted_iota(jnp.int32, (groups, chans), 1) // GROUP_SIZE
+    widen = (lax.broadcasted_iota(jnp.int32, (groups, chans), 1) // GROUP_SIZE
               == lax.broadcasted_iota(jnp.int32, (groups, chans), 0)).astype(jnp.float32)
     for kind in range(3):
-        taps[kind, 0:7, :] = jnp.dot(short_ref[kind], spread, preferred_element_type=jnp.float32,
+        taps[kind, 0:7, :] = jnp.dot(short_ref[kind], widen, preferred_element_type=jnp.float32,
                                      precision=lax.Precision.HIGHEST)
         ext[kind, HALO:, :] = feat_ref[kind].astype(jnp.float32)
 
@@ -74,7 +270,10 @@
         product[pl.ds(first + 128, 16), :] = featured(1, pl.multiple_of(first + HALO, 16), 16) * featured(2, pl.multiple_of(first + HALO, 16), 16)
         return carry
 
-    lax.fori_loop(0, rows // 16 - 1, main_rows, 0)
+    lax.fori_loop(0, 16, main_rows, 0)
+    cross_first.wait_recv()
+    spread.first()
+    lax.fori_loop(16, rows // 16 - 1, main_rows, 0)
     near.wait()
     far.wait()
     keep = (ctx > 0).astype(jnp.float32)
@@ -109,20 +308,37 @@
         return carry
 
     lax.fori_loop(0, groups, one_group, 0)
+    crossing = []
     for block in range(4):
         part = pl.ds(128 * block, 128)
         mix = mixed_t[:, part].T
         inner = product[pl.ds(128 * block + 128, 128), :].astype(jnp.bfloat16).astype(jnp.float32)
-        out_ref[part, :] = (query[part, :] * (mix + skip_ref[...] * inner)).astype(jnp.bfloat16)
-
-
-def hyena(feats, short_filter, medium_t, skip_row):
+        gated[part, :] = (query[part, :] * (mix + skip_ref[...] * inner)).astype(jnp.bfloat16)
+        crossing.append(cross(gated, gated_in, partner, g_send, g_recv, block))
+    spread.second()
+    cross_second.wait_recv()
+    later.first()
+    load_own.wait()
+    spread.finish()
+    finish = scatter_sum(gated, gated_in, crossing, base_ref, out_ref, w_own, first_half, boxes, up, down, y_pos)
+    later.second()
+    finish()
+    cross_first.wait_send()
+    cross_second.wait_send()
+    later.finish()
+
+
+def hyena(feats, short_filter, medium_t, skip_row, base, first_weight, second_weight):
     kinds, rows, chans = feats.shape
+    deep, wide = first_weight.shape
+    dma = pltpu.SemaphoreType.DMA
+    anywhere = pl.BlockSpec(memory_space=pl.ANY)
     return pl.pallas_call(
         hyena_kernel,
-        out_shape=jax.ShapeDtypeStruct((rows, chans), jnp.bfloat16),
-        in_specs=whole(4),
-        out_specs=pl.BlockSpec(memory_space=pltpu.VMEM),
+        out_shape=(jax.ShapeDtypeStruct((rows, chans), jnp.bfloat16),
+                   jax.ShapeDtypeStruct((deep, wide // 2), jnp.bfloat16)),
+        in_specs=whole(5) + [anywhere] * 2,
+        out_specs=(pl.BlockSpec(memory_space=pltpu.VMEM), anywhere),
         scratch_shapes=[
             pltpu.VMEM((3, HALO, chans), jnp.bfloat16),
             pltpu.VMEM((3, HALO + rows, chans), jnp.float32),
@@ -131,106 +347,17 @@
             pltpu.VMEM((chans, 128 + rows), jnp.bfloat16),
             pltpu.VMEM((rows, chans), jnp.float32),
             pltpu.VMEM((chans, rows), jnp.float32),
-            pltpu.SemaphoreType.DMA((2,)),
-            pltpu.SemaphoreType.DMA((2,)),
-        ],
+            dma((2,)), dma((2,)),
+            pltpu.VMEM((deep, wide // 2), jnp.bfloat16),
+            pltpu.VMEM((deep, wide // 2), jnp.bfloat16),
+            pltpu.VMEM((rows, chans), jnp.bfloat16),
+            pltpu.VMEM((rows, chans), jnp.bfloat16),
+            dma, dma((2,)), dma((2,)), dma((PIECES,)), dma((PIECES,)),
+            dma((7,)), dma((7,)), dma((7,)), dma((7,)),
+        ] + box_shapes(rows, chans),
         compiler_params=pltpu.CompilerParams(collective_id=0, has_side_effects=True, vmem_limit_bytes=VMEM_LIMIT),
         name="hyena",
-    )(feats, short_filter, medium_t, skip_row)
-
-
-def project_kernel(left_ref, base_ref, own_ref, other_ref, out_ref,
-                   w_own, w_other, left_in, outbox, inbox, kept,
-                   w_sem, x_send, x_recv, y_send, y_recv):
-    rows, depth = left_ref.shape
-    width = depth
-    ctx = lax.axis_index("ctx")
-    chan = lax.axis_index("ch")
-    y_pos = lax.rem(chan, N_Y)
-    x_lo = chan // N_Y
-    partner = (ctx, (1 - x_lo) * N_Y + y_pos)
-    column = [(ctx, x_lo * N_Y + lax.rem(y_pos + step, N_Y)) for step in range(1, N_Y)]
-    half = pl.ds(pl.multiple_of(x_lo * (N_Y * width), N_Y * width), N_Y * width)
-    load_own = pltpu.make_async_copy(own_ref.at[:, half], w_own, w_sem.at[0])
-    load_other = pltpu.make_async_copy(other_ref, w_other, w_sem.at[1])
-    load_own.start()
-    load_other.start()
-    greet([partner] + column)
-    pieces = 4
-    tall = rows // pieces
-    crossing = []
-    for piece in range(pieces):
-        part = pl.ds(piece * tall, tall)
-        copy = remote(left_ref.at[part], left_in.at[part], x_send.at[piece], x_recv.at[piece], partner)
-        copy.start()
-        crossing.append(copy)
-    load_own.wait()
-    load_other.wait()
-    sent = []
-    for piece in range(pieces):
-        part = pl.ds(piece * tall, tall)
-        crossing[piece].wait_recv()
-        mine = left_ref[part, :]
-        theirs = left_in[part, :]
-        for step in (2, 1, 3, 0):
-            target = lax.rem(y_pos + step, N_Y)
-            cols = pl.ds(pl.multiple_of(target * width, width), width)
-            term = (jnp.dot(mine, w_own[:, cols], preferred_element_type=jnp.float32)
-                    + jnp.dot(theirs, w_other[:, cols], preferred_element_type=jnp.float32))
-            if step == 0:
-                kept[part, :] = term + base_ref[part, :].astype(jnp.float32)
-            else:
-                outbox[step - 1, part, :] = term.astype(jnp.bfloat16)
-                copy = remote(outbox.at[step - 1, part], inbox.at[step - 1, part],
-                              y_send.at[step - 1, piece], y_recv.at[step - 1, piece], column[step - 1])
-                copy.start()
-                sent.append(copy)
-    for piece in range(pieces):
-        part = pl.ds(piece * tall, tall)
-        total = kept[part, :]
-        for step in (2, 1, 3):
-            sent[piece * 3 + (2, 1, 3).index(step)].wait_recv()
-            total = total + inbox[step - 1, part, :].astype(jnp.float32)
-        out_ref[part, :] = total.astype(jnp.bfloat16)
-    for copy in crossing + sent:
-        copy.wait_send()
-
-
-def project(left, base, own_weight, other_half, collective_id):
-    rows, depth = left.shape
-    width = depth
-    return pl.pallas_call(
-        project_kernel,
-        out_shape=jax.ShapeDtypeStruct((rows, width), jnp.bfloat16),
-        in_specs=whole(2) + [pl.BlockSpec(memory_space=pl.ANY)] * 2,
-        out_specs=pl.BlockSpec(memory_space=pltpu.VMEM),
-        scratch_shapes=[
-            pltpu.VMEM((depth, N_Y * width), jnp.bfloat16),
-            pltpu.VMEM((depth, N_Y * width), jnp.bfloat16),
-            pltpu.VMEM((rows, depth), jnp.bfloat16),
-            pltpu.VMEM((3, rows, width), jnp.bfloat16),
-            pltpu.VMEM((3, rows, width), jnp.bfloat16),
-            pltpu.VMEM((rows, width), jnp.float32),
-            pltpu.SemaphoreType.DMA((2,)),
-            pltpu.SemaphoreType.DMA((4,)),
-            pltpu.SemaphoreType.DMA((4,)),
-            pltpu.SemaphoreType.DMA((3, 4)),
-            pltpu.SemaphoreType.DMA((3, 4)),
-        ],
-        compiler_params=pltpu.CompilerParams(collective_id=collective_id, has_side_effects=True,
-                                             vmem_limit_bytes=VMEM_LIMIT),
-        name="project",
-    )(left, base, own_weight, other_half)
-
-
-def partner_half(weight):
-    rows, cols = weight.shape
-    chan = lax.axis_index("ch")
-    ctx = lax.axis_index("ctx")
-    x_lo = chan // N_Y
-    piece = lax.dynamic_slice(weight, (ctx * (rows // N_CTX), (1 - x_lo) * (cols // 2)), (rows // N_CTX, cols // 2))
-    piece = lax.ppermute(piece, "ch", [(source, (source + N_Y) % N_CH) for source in range(N_CH)])
-    return lax.all_gather(piece, "ctx", axis=0, tiled=True)
+    )(feats, short_filter, medium_t, skip_row, base, first_weight, second_weight)
 
 
 def qkv_kernel(stream_ref, gain_ref, cos_ref, sin_ref, w_hbm, out_ref,
@@ -367,13 +494,13 @@
         return lax.rem(z_pos + N_Z - step, N_Z)
 
     own_q = pltpu.make_async_copy(qkv_ref.at[z_pos, 0], queries.at[z_pos], own_sem.at[0])
-    own_kv = pltpu.make_async_copy(qkv_ref.at[z_pos, pl.ds(1, 2)], keyvals.at[high, z_pos, core], own_sem.at[1])
+    own_kv = pltpu.make_async_copy(qkv_ref.at[z_pos, pl.ds(1, 2)], keyvals.at[high, z_pos, :, core], own_sem.at[1])
     own_kv.start()
     own_q.start()
     z_copies, q_copies = [], []
     for step in (1, 2, 3):
         target = lax.rem(z_pos + step, N_Z)
-        copy = remote(qkv_ref.at[target, pl.ds(1, 2)], keyvals.at[high, z_pos, core],
+        copy = remote(qkv_ref.at[target, pl.ds(1, 2)], keyvals.at[high, z_pos, :, core],
                       z_send.at[step - 1], z_recv.at[step - 1], ring[step - 1])
         copy.start()
         z_copies.append(copy)
@@ -386,7 +513,7 @@
     shares, hops = [], []
 
     def spread(step):
-        place_here = keyvals.at[high, source(step), core]
+        place_here = keyvals.at[high, source(step), :, core]
         share = remote(place_here, place_here, s_send.at[step], s_recv.at[step], sibling)
         share.start()
         shares.append(share)
@@ -408,37 +535,66 @@
     for share in shares:
         share.wait_recv()
 
-    row = lax.broadcasted_iota(jnp.int32, (rows, rows), 0)
-    col = lax.broadcasted_iota(jnp.int32, (rows, rows), 1)
-    ones = jnp.ones((rows, head), jnp.bfloat16)
-
-    def update(block, x, z, c, diagonal):
-        scores = lax.dot_general(queries[block], keyvals[x, z, c, 0], (((1,), (1,)), ((), ())),
-                                 preferred_element_type=jnp.float32)
-        if diagonal:
-            scores = jnp.where(col <= row, scores, -1e30)
-        top = jnp.max(scores, axis=1, keepdims=True)
-        if not diagonal:
-            old = peak[block]
-            new = jnp.maximum(old, top)
-            peak[block] = new
-            shrink = jnp.exp2(old - new)[:, 0:1]
-        else:
-            new = jnp.broadcast_to(top, (rows, head))
-            peak[block] = new
-        weights = jnp.exp2(scores - new[:, 0:1]).astype(jnp.bfloat16)
-        wide = jnp.concatenate([keyvals[x, z, c, 1], ones], axis=1)
-        term = jnp.dot(weights, wide, preferred_element_type=jnp.float32)
-        acc[block] = term if diagonal else acc[block] * shrink + term
+    tile = 128
+    span = 2 * rows
+    row = lax.broadcasted_iota(jnp.int32, (tile, span), 0) + core * rows
+    col = lax.broadcasted_iota(jnp.int32, (tile, span), 1)
+    ones = jnp.ones((span, head), jnp.bfloat16)
+
+    def update(block, x, z, diagonal):
+        keys = keyvals[x, z, 0].reshape(span, head)
+        values = jnp.concatenate([keyvals[x, z, 1].reshape(span, head), ones], axis=1)
+        for first in range(0, rows, tile):
+            part = pl.ds(first, tile)
+            scores = lax.dot_general(queries[block, part], keys, (((1,), (1,)), ((), ())),
+                                     preferred_element_type=jnp.float32)
+            if diagonal:
+                scores = jnp.where(col <= row + first, scores, -1e30)
+            top = jnp.max(scores, axis=1, keepdims=True)
+            if diagonal:
+                new = jnp.broadcast_to(top, (tile, head))
+            else:
+                old = peak[block, part]
+                new = jnp.maximum(old, top)
+                shrink = jnp.exp2(old - new)
+            peak[block, part] = new
+            weights = jnp.exp2(scores - jnp.concatenate([new] * (span // head), axis=1)).astype(jnp.bfloat16)
+            term = jnp.dot(weights, values, preferred_element_type=jnp.float32)
+            if not diagonal:
+                term = acc[block, part] * jnp.concatenate([shrink, shrink], axis=1) + term
+            acc[block, part] = term
+
+    lanes = pl.ds(pl.multiple_of(z_pos * head, head), head)
+
+    def result_copy(block):
+        return remote(outbox.at[block], out_ref.at[:, lanes], o_send.at[block],
+                      o_recv.at[z_pos], place(high, block, core))
+
+    def complete(block):
+        result = acc[block]
+        outbox[block] = (result[:, :head] / result[:, head:]).astype(jnp.bfloat16)
+
+        @pl.when(block != z_pos)
+        def _():
+            result_copy(block).start()
+
+        @pl.when(block == z_pos)
+        def _():
+            out_ref[:, lanes] = outbox[block]
 
     def own_part(block, carry):
-        update(block, high, block, core, True)
-
-        def earlier(index, inner):
-            update(block, high, index // 2, lax.rem(index, 2), False)
+        update(block, high, block, True)
+
+        def earlier(z, inner):
+            update(block, high, z, False)
             return inner
 
-        lax.fori_loop(0, 2 * block + core, earlier, 0)
+        lax.fori_loop(0, block, earlier, 0)
+
+        @pl.when(high == 0)
+        def _():
+            complete(block)
+
         return carry
 
     lax.fori_loop(0, N_Z, own_part, 0)
@@ -448,7 +604,7 @@
         passes = []
         for order, step in enumerate((0, 1, 3, 2)):
             hops[order].wait_recv()
-            landed = keyvals.at[0, source(step), core]
+            landed = keyvals.at[0, source(step), :, core]
             copy = remote(landed, landed, t_send.at[step], t_recv.at[step], sibling)
             copy.start()
             passes.append(copy)
@@ -456,33 +612,24 @@
             copy.wait_recv()
 
         def low_part(block, carry):
-            def each(index, inner):
-                update(block, 0, index // 2, lax.rem(index, 2), False)
+            def each(z, inner):
+                update(block, 0, z, False)
                 return inner
 
-            lax.fori_loop(0, 2 * N_Z, each, 0)
+            lax.fori_loop(0, N_Z, each, 0)
+            complete(block)
             return carry
 
         lax.fori_loop(0, N_Z, low_part, 0)
         for copy in passes:
             copy.wait_send()
 
-    backs = []
-    for step in (2, 1, 3, 0):
-        target = lax.rem(z_pos + step, N_Z)
-        result = acc[target]
-        outbox[target] = (result[:, :head] / result[:, head:]).astype(jnp.bfloat16)
-        lanes = pl.ds(pl.multiple_of(z_pos * head, head), head)
-        if step == 0:
-            out_ref[:, lanes] = outbox[target]
-        else:
-            copy = remote(outbox.at[target], out_ref.at[:, lanes], o_send.at[step - 1], o_recv.at[step - 1],
-                          ring[step - 1])
-            copy.start()
-            backs.append(copy)
-    for copy in backs:
-        copy.wait_recv()
-    for copy in z_copies + q_copies + shares + backs:
+    for step in (1, 3, 2):
+        other = lax.rem(z_pos + step, N_Z)
+        landing = pl.ds(pl.multiple_of(other * head, head), head)
+        remote(outbox.at[other], out_ref.at[:, landing], o_send.at[other], o_recv.at[other],
+               place(high, other, core)).wait()
+    for copy in z_copies + q_copies + shares:
         copy.wait_send()
 
     @pl.when(high == 0)
@@ -506,7 +653,7 @@
             pltpu.VMEM((N_Z, rows, head), jnp.float32),
             pltpu.VMEM((N_Z, rows, head), jnp.bfloat16),
             dma((2,)), dma((3,)), dma((3,)), dma((3,)), dma((3,)), dma((4,)), dma((4,)),
-            dma((4,)), dma((4,)), dma((4,)), dma((4,)), dma((3,)), dma((3,)),
+            dma((4,)), dma((4,)), dma((4,)), dma((4,)), dma((4,)), dma((4,)),
         ],
         compiler_params=pltpu.CompilerParams(collective_id=3, has_side_effects=True, vmem_limit_bytes=VMEM_LIMIT),
         name="attention",
@@ -525,14 +672,12 @@
 def shards(features, residual_in, short_filter, medium_filter, skip_gain, out_weight, norm_gain, attn_weight,
            attn_out):
     rows = features.shape[0]
-    out_half = partner_half(out_weight)
-    attn_half = partner_half(attn_out)
     cosine, sine = rotation_tables(rows)
-    gated = hyena(jnp.transpose(features, (1, 0, 2)), short_filter, medium_filter.T, skip_gain[None, :])
-    stream = project(gated, residual_in, out_weight, out_half, 1)
+    stream, attn_half = hyena(jnp.transpose(features, (1, 0, 2)), short_filter, medium_filter.T,
+                              skip_gain[None, :], residual_in, out_weight, attn_out)
     qkv = gathered_qkv(stream, norm_gain[None, :], cosine, sine, attn_weight)
     attended = attention(qkv)
-    return project(attended, stream, attn_out, attn_half, 4)
+    return project(attended, stream, attn_out, attn_half)
 
 
 def solution(mesh):

time: 265 us -> 184 us (0.69)
  Pallas kernels: 216 us -> 179 us
  waiting for transfers between devices: 25.8 us -> 0 us
  between operations: 13.5 us -> 0.05 us
  local copies, waits for them, and re-layouts: 5 us -> 1.87 us
    pallas_call x1, Pallas kernels: 91.2 us -> 59.3 us  [attention(): pl.pallas_call(attention_kernel, out_shape=jax.ShapeDtypeStruct((rows, he...]
    all_gather x2 -> x0, waiting for transfers between devices: 17.9 us -> none  [partner_half(): return lax.all_gather(piece, 'ctx', axis=0, tiled=True)]
    ppermute x2 -> x0, waiting for transfers between devices: 7.81 us -> none  [partner_half(): lax.ppermute(piece, 'ch', [(source, (source + N_Y) % N_CH) for source in...]
    pallas_call x3 -> x2, Pallas kernels: 88.1 us -> 82.6 us  [the longest x1 53.9 us: hyena(): pl.pallas_call(hyena_kernel, out_shape=(jax.ShapeDtypeStruct((rows, chans...]
  transfers between devices with their start and end apart: 4 -> 0, of which waited for: 3 -> 0; matrix products, arithmetic and copies ran while one was open for 1% -> 0% of each run, Pallas kernels for 70% -> 0%
where the time goes in v2:
time: 184 us; the launch traced here: 183 us
  Pallas kernels  179 us (97%)
  other arithmetic  1.99 us (1%)
  local copies, waits for them, and re-layouts  1.87 us (1%)
    pallas_call x1, Pallas kernels, attention(): pl.pallas_call(attention_kernel, out_shape=jax.ShapeDtypeStruct((rows, he...  59.3 us
    pallas_call x1, Pallas kernels, hyena(): pl.pallas_call(hyena_kernel, out_shape=(jax.ShapeDtypeStruct((rows, chans...  53.9 us
    pallas_call x1, Pallas kernels, gathered_qkv(): pl.pallas_call(qkv_kernel, out_shape=jax.ShapeDtypeStruct((heads, 3, rows...  37.5 us
    pallas_call x1, Pallas kernels, project(): pl.pallas_call(project_kernel, out_shape=jax.ShapeDtypeStruct((rows, dept...  28.7 us

profile of v2, /device:TPU:4, one launch (start us, length us, event | category | flops | bytes accessed | tf_op | source)
XLA Modules:
  0.0 183.3 jit_solution(4214282487149510463)
XLA Ops:
  0.0 1.0 fusion
  1.0 1.0 pad_maximum_fusion
  2.0 53.9 %hyena.1 = (bf16[512,512]{1,0:T(8,128)(2,1)}, bf16[512,2048]{1,0:T(8,128)(2,1)}) custom-call(bf16[3,512,512]{2,1,0:T(8,128)(2,1)} %bitcast.4, f32[3,7,32]{2,1,0:T(8,128)} %short_ref.1, f32[32,128]{1,0:T(8,128)} %bitcast.5, f32[1,512]{1,0:T(1,128)} %bitcast.7, bf16[512,512]{1,0:T(8,128)(2,1)} %base_ref.1, bf16[512,4096]{1,0:T(8,128)(2,1)} %first_weight.1, ...), custom_call_target="tpu_custom_call" | custom-call | tf_op jit(solution)/shard_map/hyena/pallas_call | solution.py:336
  55.9 37.5 %gather_qkv.1.qkv_ref = bf16[4,3,512,128]{3,2,1,0:T(8,128)(2,1)} custom-call(bf16[512,512]{1,0:T(8,128)(2,1)} %get-tuple-element.7.stream_ref.base_ref, f32[1,4096]{1,0:T(1,128)} %bitcast.6, f32[512,128]{1,0:T(8,128)} %get-tuple-element.12.cos_ref, f32[512,128]{1,0:T(8,128)} %get-tuple-element.13.sin_ref, bf16[4096,1536]{1,0:T(8,128)(2,1)} %w_hbm.1), custom_call_target="tpu_custom_call" | custom-call | tf_op jit(solution)/shard_map/gather_qkv/pallas_call | solution.py:456
  93.4 59.3 %attention.1.left_ref = bf16[512,512]{1,0:T(8,128)(2,1)} custom-call(bf16[4,3,512,128]{3,2,1,0:T(8,128)(2,1)} %gather_qkv.1.qkv_ref), custom_call_target="tpu_custom_call" | custom-call | tf_op jit(solution)/shard_map/attention/pallas_call | solution.py:644
  152.7 28.7 %project.1 = bf16[512,512]{1,0:T(8,128)(2,1)} custom-call(bf16[512,512]{1,0:T(8,128)(2,1)} %attention.1.left_ref, bf16[512,512]{1,0:T(8,128)(2,1)} %get-tuple-element.7.stream_ref.base_ref, bf16[512,4096]{1,0:T(8,128)(2,1)} %own_ref.1, bf16[512,2048]{1,0:T(8,128)(2,1)} %get-tuple-element.8.other_ref), custom_call_target="tpu_custom_call" | custom-call | tf_op jit(solution)/shard_map/project/pallas_call | solution.py:203
  181.4 1.9 %copy.11 = bf16[512,512]{1,0:T(8,128)(2,1)} copy(bf16[512,512]{1,0:T(8,128)(2,1)} %project.1) | data formatting | bytes 1048576
  (2 shorter events, 0.0 us)

commit v3 on v2

v3 whole, which is shorter than its diff:
```python
import functools

import jax
import jax.numpy as jnp
from jax import lax
from jax.experimental import pallas as pl
from jax.experimental.pallas import tpu as pltpu
from jax.sharding import PartitionSpec as P

HEAD = 128
GROUP_SIZE = 16
N_CH = 8
N_CTX = 16
N_Y = 4
N_Z = 4
HALO = 144

norm_eps = 1e-05
MESH = pl.DeviceIdType.MESH
VMEM_LIMIT = 60 * 1024 * 1024


def remote(src, dst, send_sem, recv_sem, target):
    return pltpu.make_async_remote_copy(
        src_ref=src, dst_ref=dst, send_sem=send_sem, recv_sem=recv_sem,
        device_id=target, device_id_type=MESH,
    )


def greet(targets):
    barrier = pltpu.get_barrier_semaphore()
    for target in targets:
        pl.semaphore_signal(barrier, inc=1, device_id=target, device_id_type=MESH)
    pl.semaphore_wait(barrier, len(targets))


def whole(count):
    return [pl.BlockSpec(memory_space=pltpu.VMEM)] * count


def ring_z():
    ctx = lax.axis_index("ctx")
    chan = lax.axis_index("ch")
    core = lax.rem(ctx, 2)
    z_pos = lax.rem(ctx // 2, N_Z)
    base = ctx - z_pos * 2 - core
    sibling = (base + z_pos * 2 + 1 - core, chan)
    ring = [(base + lax.rem(z_pos + step, N_Z) * 2 + core, chan) for step in range(1, N_Z)]
    return core, z_pos, sibling, ring


def piece_rows(z_pos, core, tall):
    return pl.ds(pl.multiple_of((z_pos * 2 + core) * tall, tall), tall)


class Spread:
    def __init__(self, piece_ref, whole_ref, send_sem, recv_sem):
        self.piece, self.whole = piece_ref, whole_ref
        self.send, self.recv = send_sem, recv_sem
        self.core, self.z_pos, self.sibling, self.ring = ring_z()
        self.tall = whole_ref.shape[0] // (2 * N_Z)
        self.copies = []

    def push(self, src, rows, target):
        index = len(self.copies)
        copy = remote(src, self.whole.at[rows], self.send.at[index], self.recv.at[index], target)
        copy.start()
        self.copies.append(copy)

    def first(self):
        rows = piece_rows(self.z_pos, self.core, self.tall)
        for target in self.ring + [self.sibling]:
            self.push(self.piece, rows, target)

    def second(self):
        for step in (1, 3, 2):
            self.copies[step - 1].wait_recv()
            rows = piece_rows(lax.rem(self.z_pos + N_Z - step, N_Z), self.core, self.tall)
            self.push(self.whole.at[rows], rows, self.sibling)

    def finish(self):
        for copy in self.copies[3:]:
            copy.wait_recv()
        for copy in self.copies:
            copy.wait_send()


PIECES = 4


def column_places():
    ctx = lax.axis_index("ctx")
    chan = lax.axis_index("ch")
    y_pos = lax.rem(chan, N_Y)
    x_lo = chan // N_Y
    partner = (ctx, (1 - x_lo) * N_Y + y_pos)
    up = (ctx, x_lo * N_Y + lax.rem(y_pos + 1, N_Y))
    down = (ctx, x_lo * N_Y + lax.rem(y_pos + 3, N_Y))
    return y_pos, x_lo, partner, up, down


def piece_of(ref, piece):
    tall = ref.shape[0] // PIECES
    return ref.at[pl.ds(piece * tall, tall)]


def cross(left, left_in, partner, x_send, x_recv, piece):
    copy = remote(piece_of(left, piece), piece_of(left_in, piece), x_send.at[piece], x_recv.at[piece], partner)
    copy.start()
    return copy


def scatter_sum(left, left_in, crossing, base, out, w_own, w_other, boxes, up, down, y_pos):
    outbox, inbox, relay_out, relay_in, pending, kept, y_send, y_recv, r_send, r_recv = boxes
    rows, width = left.shape
    tall = rows // PIECES
    ways = (up, down)
    copies = []

    def term(piece, step):
        cols = pl.ds(pl.multiple_of(lax.rem(y_pos + step, N_Y) * width, width), width)
        part = pl.ds(piece * tall, tall)
        return (jnp.dot(left[part, :], w_own[:, cols], preferred_element_type=jnp.float32)
                + jnp.dot(left_in[part, :], w_other[:, cols], preferred_element_type=jnp.float32))

    def send(way, piece, value):
        outbox[way, piece] = value.astype(jnp.bfloat16)
        copy = remote(outbox.at[way, piece], inbox.at[way, piece], y_send.at[way, piece], y_recv.at[way, piece],
                      ways[way])
        copy.start()
        copies.append(copy)
        return copy

    arrivals = {}
    relays = []

    def combine(piece):
        relays[piece].wait_recv()
        way = piece % 2
        arrivals[way, piece] = send(way, piece, pending[piece] + relay_in[piece].astype(jnp.float32))

    for piece in range(PIECES):
        crossing[piece].wait_recv()
        way = piece % 2
        relay_out[piece] = term(piece, 2).astype(jnp.bfloat16)
        relay = remote(relay_out.at[piece], relay_in.at[piece], r_send.at[piece], r_recv.at[piece], ways[way])
        relay.start()
        relays.append(relay)
        arrivals[1 - way, piece] = send(1 - way, piece, term(piece, (1, 3)[1 - way]))
        pending[piece] = term(piece, (1, 3)[way])
        part = pl.ds(piece * tall, tall)
        kept[part, :] = term(piece, 0) + base[part, :].astype(jnp.float32)
        if piece:
            combine(piece - 1)
    combine(PIECES - 1)

    def finish():
        for piece in range(PIECES):
            part = pl.ds(piece * tall, tall)
            for way in (1 - piece % 2, piece % 2):
                arrivals[way, piece].wait_recv()
            total = kept[part, :] + inbox[0, piece].astype(jnp.float32) + inbox[1, piece].astype(jnp.float32)
            out[part, :] = total.astype(jnp.bfloat16)
        for copy in list(crossing) + copies + relays:
            copy.wait_send()

    return finish


def box_shapes(rows, width):
    tall = rows // PIECES
    dma = pltpu.SemaphoreType.DMA
    return [
        pltpu.VMEM((2, PIECES, tall, width), jnp.bfloat16),
        pltpu.VMEM((2, PIECES, tall, width), jnp.bfloat16),
        pltpu.VMEM((PIECES, tall, width), jnp.bfloat16),
        pltpu.VMEM((PIECES, tall, width), jnp.bfloat16),
        pltpu.VMEM((PIECES, tall, width), jnp.float32),
        pltpu.VMEM((rows, width), jnp.float32),
        dma((2, PIECES)), dma((2, PIECES)), dma((PIECES,)), dma((PIECES,)),
    ]


def hyena_kernel(feat_ref, short_ref, medium_ref, skip_ref, base_ref, first_weight, second_weight,
                 out_ref, second_half,
                 halo, ext, taps, product, product_t, query, mixed_t, send_sem, recv_sem,
                 w_own, first_half, gated, gated_in, w_sem, x_send, x_recv, g_send, g_recv,
                 w_send, w_recv, v_send, v_recv, *boxes):
    rows, chans = out_ref.shape
    ctx = lax.axis_index("ctx")
    chan = lax.axis_index("ch")
    after = (lax.rem(ctx + 1, N_CTX), chan)
    before = (lax.rem(ctx + N_CTX - 1, N_CTX), chan)
    y_pos, x_lo, partner, up, down = column_places()
    core, z_pos, sibling, ring = ring_z()
    span = first_half.shape[1]
    load_own = pltpu.make_async_copy(
        first_weight.at[:, pl.ds(pl.multiple_of(x_lo * span, span), span)], w_own, w_sem)
    load_own.start()
    greet([after, before, partner, sibling, up, down] + ring)
    near = remote(feat_ref.at[pl.ds(0, 1), pl.ds(rows - 16, 16)], halo.at[pl.ds(0, 1), pl.ds(HALO - 16, 16)],
                  send_sem.at[0], recv_sem.at[0], after)
    far = remote(feat_ref.at[pl.ds(1, 2), pl.ds(rows - HALO, HALO)], halo.at[pl.ds(1, 2)],
                 send_sem.at[1], recv_sem.at[1], after)
    near.start()
    far.start()
    tall = first_half.shape[0] // (2 * N_Z)
    mine = piece_rows(z_pos, core, tall)
    half = pl.ds(pl.multiple_of((1 - x_lo) * span, span), span)
    cross_first = remote(first_weight.at[mine, half], first_half.at[mine], x_send.at[0], x_recv.at[0], partner)
    cross_second = remote(second_weight.at[mine, half], second_half.at[mine], x_send.at[1], x_recv.at[1], partner)
    cross_first.start()
    spread = Spread(first_half.at[mine], first_half, w_send, w_recv)
    later = Spread(second_half.at[mine], second_half, v_send, v_recv)

    groups = short_ref.shape[2]
    widen = (lax.broadcasted_iota(jnp.int32, (groups, chans), 1) // GROUP_SIZE
              == lax.broadcasted_iota(jnp.int32, (groups, chans), 0)).astype(jnp.float32)
    for kind in range(3):
        taps[kind, 0:7, :] = jnp.dot(short_ref[kind], widen, preferred_element_type=jnp.float32,
                                     precision=lax.Precision.HIGHEST)
        ext[kind, HALO:, :] = feat_ref[kind].astype(jnp.float32)

    def featured(kind, first, count):
        slab = ext[kind, pl.ds(first - 8 if isinstance(first, int) else pl.multiple_of(first - 8, 8), count + 8), :]
        total = taps[kind, 0:1, :] * slab[8:]
        for tap in range(1, 7):
            total = total + taps[kind, tap : tap + 1, :] * pltpu.roll(slab, tap, 0)[8:]
        return total

    def main_rows(step, carry):
        first = pl.multiple_of(16 + step * 16, 16)
        query[pl.ds(first, 16), :] = featured(0, pl.multiple_of(first + HALO, 16), 16)
        product[pl.ds(first + 128, 16), :] = featured(1, pl.multiple_of(first + HALO, 16), 16) * featured(2, pl.multiple_of(first + HALO, 16), 16)
        return carry

    lax.fori_loop(0, 8, main_rows, 0)
    cross_first.wait_recv()
    spread.first()
    cross_second.start()
    lax.fori_loop(8, rows // 16 - 1, main_rows, 0)
    near.wait()
    far.wait()
    keep = (ctx > 0).astype(jnp.float32)
    ext[0, HALO - 16 : HALO, :] = halo[0, HALO - 16 : HALO, :].astype(jnp.float32) * keep
    for kind in (1, 2):
        ext[kind, 0:HALO, :] = halo[kind].astype(jnp.float32) * keep
    query[0:16, :] = featured(0, HALO, 16)

    def rim_rows(step, carry):
        first = pl.multiple_of(step * 16, 16)
        product[pl.ds(first, 16), :] = featured(1, pl.multiple_of(first + 16, 16), 16) * featured(2, pl.multiple_of(first + 16, 16), 16)
        return carry

    lax.fori_loop(0, 9, rim_rows, 0)
    for block in range(5):
        product_t[:, 128 * block : 128 * block + 128] = (
            product[128 * block : 128 * block + 128, :].T.astype(jnp.bfloat16))
    row = lax.broadcasted_iota(jnp.int32, (128, 128), 0)
    col = lax.broadcasted_iota(jnp.int32, (128, 128), 1)

    def one_group(group, carry):
        line = jnp.broadcast_to(medium_ref[pl.ds(group, 1), :], (128, 128))
        wheel = pltpu.roll(line, 0, 1, stride=1, stride_axis=0)
        table = jnp.concatenate([jnp.where(col < row, wheel, 0.0), jnp.where(col >= row, wheel, 0.0)],
                                axis=0).astype(jnp.bfloat16)
        lane = pl.ds(pl.multiple_of(group * GROUP_SIZE, GROUP_SIZE), GROUP_SIZE)
        window = jnp.concatenate(
            [product_t[lane, 128 * block : 128 * block + 256] for block in range(4)], axis=0)
        mix = jnp.dot(window, table, preferred_element_type=jnp.float32)
        for block in range(4):
            mixed_t[lane, 128 * block : 128 * block + 128] = mix[16 * block : 16 * block + 16, :]
        return carry

    lax.fori_loop(0, groups, one_group, 0)
    crossing = []
    for block in range(4):
        part = pl.ds(128 * block, 128)
        mix = mixed_t[:, part].T
        inner = product[pl.ds(128 * block + 128, 128), :].astype(jnp.bfloat16).astype(jnp.float32)
        gated[part, :] = (query[part, :] * (mix + skip_ref[...] * inner)).astype(jnp.bfloat16)
        crossing.append(cross(gated, gated_in, partner, g_send, g_recv, block))
    spread.second()
    cross_second.wait_recv()
    later.first()
    load_own.wait()
    spread.finish()
    finish = scatter_sum(gated, gated_in, crossing, base_ref, out_ref, w_own, first_half, boxes, up, down, y_pos)
    later.second()
    finish()
    cross_first.wait_send()
    cross_second.wait_send()
    later.finish()


def hyena(feats, short_filter, medium_t, skip_row, base, first_weight, second_weight):
    kinds, rows, chans = feats.shape
    deep, wide = first_weight.shape
    dma = pltpu.SemaphoreType.DMA
    anywhere = pl.BlockSpec(memory_space=pl.ANY)
    return pl.pallas_call(
        hyena_kernel,
        out_shape=(jax.ShapeDtypeStruct((rows, chans), jnp.bfloat16),
                   jax.ShapeDtypeStruct((deep, wide // 2), jnp.bfloat16)),
        in_specs=whole(5) + [anywhere] * 2,
        out_specs=(pl.BlockSpec(memory_space=pltpu.VMEM), anywhere),
        scratch_shapes=[
            pltpu.VMEM((3, HALO, chans), jnp.bfloat16),
            pltpu.VMEM((3, HALO + rows, chans), jnp.float32),
            pltpu.VMEM((3, 8, chans), jnp.float32),
            pltpu.VMEM((128 + rows, chans), jnp.float32),
            pltpu.VMEM((chans, 128 + rows), jnp.bfloat16),
            pltpu.VMEM((rows, chans), jnp.float32),
            pltpu.VMEM((chans, rows), jnp.float32),
            dma((2,)), dma((2,)),
            pltpu.VMEM((deep, wide // 2), jnp.bfloat16),
            pltpu.VMEM((deep, wide // 2), jnp.bfloat16),
            pltpu.VMEM((rows, chans), jnp.bfloat16),
            pltpu.VMEM((rows, chans), jnp.bfloat16),
            dma, dma((2,)), dma((2,)), dma((PIECES,)), dma((PIECES,)),
            dma((7,)), dma((7,)), dma((7,)), dma((7,)),
        ] + box_shapes(rows, chans),
        compiler_params=pltpu.CompilerParams(collective_id=0, has_side_effects=True, vmem_limit_bytes=VMEM_LIMIT),
        name="hyena",
    )(feats, short_filter, medium_t, skip_row, base, first_weight, second_weight)


def attention_kernel(stream_ref, gain_ref, cos_ref, sin_ref, weight_ref, own_ref, other_ref, out_ref,
                     blocks, w_ref, wide_acc, squares, qkv,
                     queries, keyvals, acc, peak, results, attended, attended_in, w_own, w_other,
                     outbox, inbox, relay_out, relay_in, pending, kept,
                     y_send, y_recv, r_send, r_recv,
                     w_sem, g_send, g_recv, own_sem, q_send, q_recv, z_send, z_recv, s_send, s_recv,
                     h_send, h_recv, t_send, t_recv, o_send, o_recv, p_send, p_recv):
    rows, width = stream_ref.shape
    head = HEAD
    heads = width // head
    tile = rows // PIECES
    tall = rows // 2
    ctx = lax.axis_index("ctx")
    core = lax.rem(ctx, 2)
    z_pos = lax.rem(ctx // 2, N_Z)
    high = ctx // (2 * N_Z)
    chan = lax.axis_index("ch")
    y_pos, x_lo, partner, dev_up, dev_down = column_places()
    up, down, opposite = lax.rem(y_pos + 1, N_Y), lax.rem(y_pos + 3, N_Y), lax.rem(y_pos + 2, N_Y)
    wide = w_own.shape[1]
    loads = [
        pltpu.make_async_copy(weight_ref, w_ref, w_sem.at[0]),
        pltpu.make_async_copy(own_ref.at[:, pl.ds(pl.multiple_of(x_lo * wide, wide), wide)], w_own, w_sem.at[1]),
        pltpu.make_async_copy(other_ref, w_other, w_sem.at[2]),
    ]
    for load in loads:
        load.start()

    def place(x, z, c):
        return ((x * N_Z + z) * 2 + c, chan)

    def partner_place(z):
        return ((high * N_Z + z) * 2 + core, (1 - x_lo) * N_Y + y_pos)

    sibling = place(high, z_pos, 1 - core)
    across = place(1 - high, z_pos, core)
    others = [lax.rem(z_pos + step, N_Z) for step in range(1, N_Z)]
    ring = [place(high, z, core) for z in others]
    greet([dev_up, dev_down, partner, sibling, across] + ring + [partner_place(z) for z in others])

    def slot(x, y):
        return x * N_Y + y

    halves = [pl.ds(0, tall), pl.ds(tall, tall)]
    quarters = [[pl.ds(half * tall + number * (tall // 2), tall // 2) for number in range(2)] for half in range(2)]
    sent = {}

    def push(name, src, where, part, target):
        index = len(sent)
        copy = remote(src.at[part], blocks.at[where, part], g_send.at[index], g_recv.at[index], target)
        copy.start()
        sent[name] = copy

    mine, other = slot(x_lo, y_pos), slot(1 - x_lo, y_pos)
    above, below, far = slot(x_lo, up), slot(x_lo, down), slot(x_lo, opposite)

    def own_sends(half):
        part = halves[half]
        push(("x", half), stream_ref, mine, part, partner)
        push(("up", half), stream_ref, mine, part, dev_up)
        push(("down", half), stream_ref, mine, part, dev_down)

    def pass_on(half):
        first, second = quarters[half]
        part = halves[half]
        sent["up", half].wait_recv()
        push(("upup", half), blocks.at[below], below, first, dev_up)
        sent["down", half].wait_recv()
        push(("downdown", half), blocks.at[above], above, second, dev_down)
        sent["x", half].wait_recv()
        push(("xup", half), blocks.at[other], other, part, dev_up)
        push(("xdown", half), blocks.at[other], other, part, dev_down)

    def pass_far(half):
        first, second = quarters[half]
        sent["upup", half].wait_recv()
        push(("far0", half), blocks.at[far], far, first, partner)
        sent["downdown", half].wait_recv()
        push(("far1", half), blocks.at[far], far, second, partner)

    def use(src, where, half, fresh=False):
        part = halves[half]
        value = src[part, :].astype(jnp.float32)
        square = value * value
        partial = (square[:, 0:128] + square[:, 128:256]) + (square[:, 256:384] + square[:, 384:512])
        cols = pl.ds(pl.multiple_of(where * width, width), width)
        scaled = (value * gain_ref[:, cols]).astype(jnp.bfloat16)
        term = jnp.dot(scaled, w_ref[cols, :], preferred_element_type=jnp.float32)
        squares[part, :] = partial if fresh else squares[part, :] + partial
        wide_acc[part, :] = term if fresh else wide_acc[part, :] + term

    def last_uses(half):
        for names, y in ((("xdown",), up), (("xup",), down), (("far0", "far1"), opposite)):
            for name in names:
                sent[name, half].wait_recv()
            use(blocks.at[slot(1 - x_lo, y)], slot(1 - x_lo, y), half)

    scale = head ** -0.5 * 1.4426950408889634

    def heads_out(half):
        part = halves[half]
        inverse = lax.rsqrt(jnp.sum(squares[part, :], axis=1, keepdims=True) / (N_CH * width) + norm_eps)
        for number in range(heads):
            for kind in range(3):
                first = (number * 3 + kind) * head
                value = wide_acc[part, first : first + head] * inverse
                if kind < 2:
                    value = value * cos_ref[part, :] + pltpu.roll(value, head // 2, 1) * sin_ref[part, :]
                if kind == 0:
                    value = value * scale
                qkv[number, kind, part, :] = value.astype(jnp.bfloat16)

    z_copies, q_copies, own_copies = {}, {}, []

    def exchange(half):
        part = halves[half]
        own_kv = pltpu.make_async_copy(qkv.at[z_pos, pl.ds(1, 2), part],
                                       keyvals.at[high, z_pos, :, core, part], own_sem.at[half, 1])
        own_q = pltpu.make_async_copy(qkv.at[z_pos, 0, part], queries.at[z_pos, part], own_sem.at[half, 0])
        own_kv.start()
        own_q.start()
        own_copies.append((own_kv, own_q))
        for step in (1, 2, 3):
            copy = remote(qkv.at[others[step - 1], pl.ds(1, 2), part], keyvals.at[high, z_pos, :, core, part],
                          z_send.at[half, step - 1], z_recv.at[half, step - 1], ring[step - 1])
            copy.start()
            z_copies[half, step] = copy
        for step in (1, 2, 3):
            copy = remote(qkv.at[others[step - 1], 0, part], queries.at[z_pos, part],
                          q_send.at[half, step - 1], q_recv.at[half, step - 1], ring[step - 1])
            copy.start()
            q_copies[half, step] = copy

    own_sends(0)
    loads[0].wait()
    use(stream_ref, mine, 0, True)
    pass_on(0)
    own_sends(1)
    use(blocks.at[above], above, 0)
    use(blocks.at[below], below, 0)
    use(blocks.at[other], other, 0)
    pass_far(0)
    use(blocks.at[far], far, 0)
    use(stream_ref, mine, 1, True)
    last_uses(0)
    heads_out(0)
    exchange(0)
    pass_on(1)
    use(blocks.at[above], above, 1)
    use(blocks.at[below], below, 1)
    pass_far(1)
    use(blocks.at[other], other, 1)
    use(blocks.at[far], far, 1)
    last_uses(1)
    heads_out(1)
    exchange(1)

    def source(step):
        return lax.rem(z_pos + N_Z - step, N_Z)

    shares, hops = [], []

    def spread(step, half):
        index = len(shares)
        place_here = keyvals.at[high, source(step), :, core, halves[half]]
        share = remote(place_here, place_here, s_send.at[index], s_recv.at[index], sibling)
        share.start()
        shares.append(share)
        hop = remote(place_here, place_here, h_send.at[index], h_recv.at[index], across)
        hops.append(hop)

        @pl.when(high == 0)
        def _():
            hop.start()

    order = [(step, half) for half in range(2) for step in (0, 1, 3, 2)]
    for step, half in order:
        if step:
            z_copies[half, step].wait_recv()
        else:
            own_copies[half][0].wait()
        spread(step, half)
    for pair in own_copies:
        pair[1].wait()
    for copy in list(q_copies.values()) + shares:
        copy.wait_recv()

    span = 2 * rows
    row = lax.broadcasted_iota(jnp.int32, (tile, span), 0) + core * rows
    col = lax.broadcasted_iota(jnp.int32, (tile, span), 1)
    ones = jnp.ones((span, head), jnp.bfloat16)

    def piece_at(piece):
        return pl.ds(pl.multiple_of(piece * tile, tile), tile)

    def update(block, part, first, x, z, diagonal):
        keys = keyvals[x, z, 0].reshape(span, head)
        values = jnp.concatenate([keyvals[x, z, 1].reshape(span, head), ones], axis=1)
        scores = lax.dot_general(queries[block, part], keys, (((1,), (1,)), ((), ())),
                                 preferred_element_type=jnp.float32)
        if diagonal:
            scores = jnp.where(col <= row + first, scores, -1e30)
        top = jnp.max(scores, axis=1, keepdims=True)
        if diagonal:
            new = jnp.broadcast_to(top, (tile, head))
        else:
            old = peak[block, part]
            new = jnp.maximum(old, top)
            shrink = jnp.exp2(old - new)
        peak[block, part] = new
        weights = jnp.exp2(scores - jnp.concatenate([new] * (span // head), axis=1)).astype(jnp.bfloat16)
        term = jnp.dot(weights, values, preferred_element_type=jnp.float32)
        if not diagonal:
            term = acc[block, part] * jnp.concatenate([shrink, shrink], axis=1) + term
        acc[block, part] = term

    def own_tile(piece):
        part, first = piece_at(piece), piece * tile
        for block in range(N_Z):
            update(block, part, first, high, block, True)
        for z in range(N_Z - 1):
            for block in range(z + 1, N_Z):
                update(block, part, first, high, z, False)

    def low_tile(piece):
        part, first = piece_at(piece), piece * tile

        def each(z, carry):
            for block in range(N_Z):
                update(block, part, first, 0, z, False)
            return carry

        lax.fori_loop(0, N_Z, each, 0)

    lanes = pl.ds(pl.multiple_of(z_pos * head, head), head)

    def result_copy(piece, block, owner):
        columns = pl.ds(pl.multiple_of(owner * head, head), head)
        part = piece_at(piece)
        return remote(results.at[block, part], attended.at[part, columns], o_send.at[piece, block],
                      o_recv.at[piece, owner], place(high, block, core))

    def partner_copy(piece, block, owner):
        columns = pl.ds(pl.multiple_of(owner * head, head), head)
        part = piece_at(piece)
        return remote(results.at[block, part], attended_in.at[part, columns], p_send.at[piece, block],
                      p_recv.at[piece, owner], partner_place(block))

    def complete(piece):
        part = piece_at(piece)

        def each(block, carry):
            total = acc[block, part]
            results[block, part] = (total[:, :head] / total[:, head:]).astype(jnp.bfloat16)
            partner_copy(piece, block, z_pos).start()

            @pl.when(block != z_pos)
            def _():
                result_copy(piece, block, z_pos).start()

            @pl.when(block == z_pos)
            def _():
                attended[part, lanes] = results[block, part]

            return carry

        lax.fori_loop(0, N_Z, each, 0)

    def way_place(way):
        return (ctx, x_lo * N_Y + lax.rem(y_pos + 1 + 2 * way, N_Y))

    def relay_copy(piece):
        return remote(relay_out.at[piece], relay_in.at[piece], r_send.at[piece], r_recv.at[piece],
                      way_place(lax.rem(piece, 2)))

    def direct_copy(way, piece):
        return remote(outbox.at[way, piece], inbox.at[way, piece], y_send.at[way, piece], y_recv.at[way, piece],
                      way_place(way))

    def multiply(piece):
        for z in others:
            result_copy(piece, z, z).wait_recv()
        for z in others + [z_pos]:
            partner_copy(piece, z, z).wait_recv()
        part = piece_at(piece)
        mine, theirs = attended[part, :], attended_in[part, :]

        def term(step):
            cols = pl.ds(pl.multiple_of(lax.rem(y_pos + step, N_Y) * width, width), width)
            return (jnp.dot(mine, w_own[:, cols], preferred_element_type=jnp.float32)
                    + jnp.dot(theirs, w_other[:, cols], preferred_element_type=jnp.float32))

        way = lax.rem(piece, 2)
        relay_out[piece] = term(2).astype(jnp.bfloat16)
        relay_copy(piece).start()
        outbox[1 - way, piece] = term(3 - 2 * way).astype(jnp.bfloat16)
        direct_copy(1 - way, piece).start()
        pending[piece] = term(1 + 2 * way)
        kept[part, :] = term(0) + stream_ref[part, :].astype(jnp.float32)

    def combine(piece):
        relay_copy(piece).wait_recv()
        way = lax.rem(piece, 2)
        outbox[way, piece] = (pending[piece] + relay_in[piece].astype(jnp.float32)).astype(jnp.bfloat16)
        direct_copy(way, piece).start()

    @pl.when(high == 1)
    def _():
        def each(piece, carry):
            own_tile(piece)
            return carry

        lax.fori_loop(0, PIECES, each, 0)
        passes = []
        for index, (step, half) in enumerate(order):
            hops[index].wait_recv()
            landed = keyvals.at[0, source(step), :, core, halves[half]]
            copy = remote(landed, landed, t_send.at[index], t_recv.at[index], sibling)
            copy.start()
            passes.append(copy)
        for copy in passes:
            copy.wait()

    loads[1].wait()
    loads[2].wait()

    def stage(step, carry):
        @pl.when(step < PIECES)
        def _():
            @pl.when(high == 0)
            def _():
                own_tile(step)

            @pl.when(high == 1)
            def _():
                low_tile(step)

            complete(step)

        @pl.when(jnp.logical_and(step >= 1, step <= PIECES))
        def _():
            multiply(step - 1)

        @pl.when(step >= 2)
        def _():
            combine(step - 2)

        return carry

    lax.fori_loop(0, PIECES + 2, stage, 0)

    def finish(piece, carry):
        part = piece_at(piece)
        direct_copy(0, piece).wait_recv()
        direct_copy(1, piece).wait_recv()
        total = kept[part, :] + inbox[0, piece].astype(jnp.float32) + inbox[1, piece].astype(jnp.float32)
        out_ref[part, :] = total.astype(jnp.bfloat16)
        return carry

    lax.fori_loop(0, PIECES, finish, 0)

    def drain(piece, carry):
        for z in others:
            result_copy(piece, z, z_pos).wait_send()
        for z in others + [z_pos]:
            partner_copy(piece, z, z_pos).wait_send()
        relay_copy(piece).wait_send()
        direct_copy(0, piece).wait_send()
        direct_copy(1, piece).wait_send()
        return carry

    lax.fori_loop(0, PIECES, drain, 0)
    for copy in list(sent.values()) + list(z_copies.values()) + list(q_copies.values()) + shares:
        copy.wait_send()

    @pl.when(high == 0)
    def _():
        for hop in hops:
            hop.wait_send()


def attention(stream, gain_row, cosine, sine, weight, own_weight, other_half):
    rows, width = stream.shape
    head = HEAD
    dma = pltpu.SemaphoreType.DMA
    return pl.pallas_call(
        attention_kernel,
        out_shape=jax.ShapeDtypeStruct((rows, width), jnp.bfloat16),
        in_specs=whole(4) + [pl.BlockSpec(memory_space=pl.ANY)] * 3,
        out_specs=pl.BlockSpec(memory_space=pltpu.VMEM),
        scratch_shapes=[
            pltpu.VMEM((N_CH, rows, width), jnp.bfloat16),
            pltpu.VMEM(weight.shape, jnp.bfloat16),
            pltpu.VMEM((rows, weight.shape[1]), jnp.float32),
            pltpu.VMEM((rows, 128), jnp.float32),
            pltpu.VMEM((width // head, 3, rows, head), jnp.bfloat16),
            pltpu.VMEM((N_Z, rows, head), jnp.bfloat16),
            pltpu.VMEM((2, N_Z, 2, 2, rows, head), jnp.bfloat16),
            pltpu.VMEM((N_Z, rows, 2 * head), jnp.float32),
            pltpu.VMEM((N_Z, rows, head), jnp.float32),
            pltpu.VMEM((N_Z, rows, head), jnp.bfloat16),
            pltpu.VMEM((rows, width), jnp.bfloat16),
            pltpu.VMEM((rows, width), jnp.bfloat16),
            pltpu.VMEM((width, N_Y * width), jnp.bfloat16),
            pltpu.VMEM((width, N_Y * width), jnp.bfloat16),
        ] + box_shapes(rows, width) + [
            dma((3,)), dma((18,)), dma((18,)), dma((2, 2)), dma((2, 3)), dma((2, 3)), dma((2, 3)), dma((2, 3)),
            dma((8,)), dma((8,)), dma((8,)), dma((8,)), dma((8,)), dma((8,)),
            dma((PIECES, N_Z)), dma((PIECES, N_Z)), dma((PIECES, N_Z)), dma((PIECES, N_Z)),
        ],
        compiler_params=pltpu.CompilerParams(collective_id=3, has_side_effects=True, vmem_limit_bytes=VMEM_LIMIT),
        name="attention",
    )(stream, gain_row, cosine, sine, weight, own_weight, other_half)


def rotation_tables(rows):
    positions = lax.axis_index("ctx") * rows + jnp.arange(rows, dtype=jnp.int32)
    half_size = HEAD // 2
    frequency = 10000.0 ** (-jnp.arange(half_size, dtype=jnp.float32) * 2.0 / HEAD)
    angles = positions.astype(jnp.float32)[:, None] * frequency[None, :]
    cosine, sine = jnp.cos(angles), jnp.sin(angles)
    return jnp.concatenate([cosine, cosine], axis=1), jnp.concatenate([-sine, sine], axis=1)


def shards(features, residual_in, short_filter, medium_filter, skip_gain, out_weight, norm_gain, attn_weight,
           attn_out):
    rows = features.shape[0]
    cosine, sine = rotation_tables(rows)
    stream, attn_half = hyena(jnp.transpose(features, (1, 0, 2)), short_filter, medium_filter.T,
                              skip_gain[None, :], residual_in, out_weight, attn_out)
    return attention(stream, norm_gain[None, :], cosine, sine, attn_weight, attn_out, attn_half)


def solution(mesh):
    in_specs = (
        P("ctx", None, "ch"),
        P("ctx", "ch"),
        P(None, None, "ch"),
        P(None, "ch"),
        P("ch"),
        P("ch", None),
        P(),
        P(None, "ch"),
        P("ch", None),
    )
    out_specs = P("ctx", "ch")
    return jax.shard_map(shards, mesh=mesh, in_specs=in_specs, out_specs=out_specs, check_vma=False)
```

time: 184 us -> 161 us (0.88)
  Pallas kernels: 179 us -> 157 us
    pallas_call x3 -> x1, Pallas kernels: 125 us -> 103 us  [attention(): pl.pallas_call(attention_kernel, out_shape=jax.ShapeDtypeStruct((rows, wi...]
where the time goes in v3:
time: 161 us
  Pallas kernels  157 us (98%)
  other arithmetic  2 us (1%)
  local copies, waits for them, and re-layouts  1.87 us (1%)
    pallas_call x1, Pallas kernels, attention(): pl.pallas_call(attention_kernel, out_shape=jax.ShapeDtypeStruct((rows, wi...  103 us
    pallas_call x1, Pallas kernels, hyena(): pl.pallas_call(hyena_kernel, out_shape=(jax.ShapeDtypeStruct((rows, chans...  53.8 us

profile of v3, /device:TPU:4, one launch (start us, length us, event | category | flops | bytes accessed | tf_op | source)
XLA Modules:
  0.0 160.7 jit_solution(8055986024584620037)
XLA Ops:
  0.0 1.0 fusion
  1.0 1.0 pad_maximum_fusion
  2.0 53.8 %hyena.1 = (bf16[512,512]{1,0:T(8,128)(2,1)}, bf16[512,2048]{1,0:T(8,128)(2,1)}) custom-call(bf16[3,512,512]{2,1,0:T(8,128)(2,1)} %bitcast.4, f32[3,7,32]{2,1,0:T(8,128)} %short_ref.1, f32[32,128]{1,0:T(8,128)} %bitcast.5, f32[1,512]{1,0:T(1,128)} %bitcast.7, bf16[512,512]{1,0:T(8,128)(2,1)} %base_ref.1, bf16[512,4096]{1,0:T(8,128)(2,1)} %first_weight.1, ...), custom_call_target="tpu_custom_call" | custom-call | tf_op jit(solution)/shard_map/hyena/pallas_call | solution.py:301
  55.9 103.0 %attention.1 = bf16[512,512]{1,0:T(8,128)(2,1)} custom-call(bf16[512,512]{1,0:T(8,128)(2,1)} %get-tuple-element.7.stream_ref, f32[1,4096]{1,0:T(1,128)} %bitcast.6, f32[512,128]{1,0:T(8,128)} %get-tuple-element.12.cos_ref, f32[512,128]{1,0:T(8,128)} %get-tuple-element.13.sin_ref, bf16[4096,1536]{1,0:T(8,128)(2,1)} %weight_ref.1, bf16[512,4096]{1,0:T(8,128)(2,1)} %own_ref.1, ...), custom_call_target="tpu_custom_call" | custom-call | tf_op jit(solution)/shard_map/attention/pallas_call | solution.py:713
  158.9 1.9 %copy.11 = bf16[512,512]{1,0:T(8,128)(2,1)} copy(bf16[512,512]{1,0:T(8,128)(2,1)} %attention.1) | data formatting | bytes 1048576
  (2 shorter events, 0.0 us)

commit v4 on v3

--- a/solution.py
+++ b/solution.py
@@ -331,7 +331,7 @@
                      outbox, inbox, relay_out, relay_in, pending, kept,
                      y_send, y_recv, r_send, r_recv,
                      w_sem, g_send, g_recv, own_sem, q_send, q_recv, z_send, z_recv, s_send, s_recv,
-                     h_send, h_recv, t_send, t_recv, o_send, o_recv, p_send, p_recv):
+                     h_send, h_recv, t_send, t_recv, o_send, o_recv, p_send, p_recv, transit, d_send, d_recv):
     rows, width = stream_ref.shape
     head = HEAD
     heads = width // head
@@ -363,7 +363,8 @@
     across = place(1 - high, z_pos, core)
     others = [lax.rem(z_pos + step, N_Z) for step in range(1, N_Z)]
     ring = [place(high, z, core) for z in others]
-    greet([dev_up, dev_down, partner, sibling, across] + ring + [partner_place(z) for z in others])
+    diagonal = (((1 - high) * N_Z + z_pos) * 2 + core, (1 - x_lo) * N_Y + y_pos)
+    greet([dev_up, dev_down, partner, sibling, across, diagonal] + ring + [partner_place(z) for z in others])
 
     def slot(x, y):
         return x * N_Y + y
@@ -493,7 +494,10 @@
         share = remote(place_here, place_here, s_send.at[index], s_recv.at[index], sibling)
         share.start()
         shares.append(share)
-        hop = remote(place_here, place_here, h_send.at[index], h_recv.at[index], across)
+        if half == 0:
+            hop = remote(place_here, place_here, h_send.at[index], h_recv.at[index], across)
+        else:
+            hop = remote(place_here, transit.at[step], h_send.at[index], h_recv.at[index], diagonal)
         hops.append(hop)
 
         @pl.when(high == 0)
@@ -520,9 +524,11 @@
     def piece_at(piece):
         return pl.ds(pl.multiple_of(piece * tile, tile), tile)
 
-    def update(block, part, first, x, z, diagonal):
-        keys = keyvals[x, z, 0].reshape(span, head)
-        values = jnp.concatenate([keyvals[x, z, 1].reshape(span, head), ones], axis=1)
+    def update(block, part, first, z, diagonal):
+        fold(block, part, first, keyvals[high, z, 0].reshape(span, head), keyvals[high, z, 1].reshape(span, head), diagonal)
+
+    def fold(block, part, first, keys, plain_values, diagonal):
+        values = jnp.concatenate([plain_values, ones], axis=1)
         scores = lax.dot_general(queries[block, part], keys, (((1,), (1,)), ((), ())),
                                  preferred_element_type=jnp.float32)
         if diagonal:
@@ -544,20 +550,25 @@
     def own_tile(piece):
         part, first = piece_at(piece), piece * tile
         for block in range(N_Z):
-            update(block, part, first, high, block, True)
+            update(block, part, first, block, True)
         for z in range(N_Z - 1):
             for block in range(z + 1, N_Z):
-                update(block, part, first, high, z, False)
-
-    def low_tile(piece):
+                update(block, part, first, z, False)
+
+    def low_tile(piece, half):
         part, first = piece_at(piece), piece * tile
 
-        def each(z, carry):
+        def each(pair, carry):
+            keys, values = [
+                jnp.concatenate([keyvals[0, 2 * pair + number, kind, side, halves[half], :]
+                                 for number in range(2) for side in range(2)], axis=0)
+                for kind in range(2)
+            ]
             for block in range(N_Z):
-                update(block, part, first, 0, z, False)
+                fold(block, part, first, keys, values, False)
             return carry
 
-        lax.fori_loop(0, N_Z, each, 0)
+        lax.fori_loop(0, N_Z // 2, each, 0)
 
     lanes = pl.ds(pl.multiple_of(z_pos * head, head), head)
 
@@ -633,20 +644,44 @@
 
     @pl.when(high == 1)
     def _():
-        def each(piece, carry):
-            own_tile(piece)
-            return carry
-
-        lax.fori_loop(0, PIECES, each, 0)
-        passes = []
-        for index, (step, half) in enumerate(order):
-            hops[index].wait_recv()
-            landed = keyvals.at[0, source(step), :, core, halves[half]]
-            copy = remote(landed, landed, t_send.at[index], t_recv.at[index], sibling)
+        passes, legs = [], []
+
+        def landed(index):
+            step, half = order[index]
+            return keyvals.at[0, source(step), :, core, halves[half]]
+
+        def forward(index):
+            copy = remote(landed(index), landed(index), t_send.at[index], t_recv.at[index], sibling)
             copy.start()
             passes.append(copy)
+
+        for index in range(4):
+            hops[index].wait_recv()
+            forward(index)
+        for index in range(4, 8):
+            own_tile(index - 4)
+            hops[index].wait_recv()
+            leg = remote(transit.at[order[index][0]], landed(index), d_send.at[index - 4], d_recv.at[index - 4], partner)
+            leg.start()
+            legs.append(leg)
         for copy in passes:
-            copy.wait()
+            copy.wait_recv()
+
+        def each(piece, carry):
+            low_tile(piece, 0)
+            return carry
+
+        lax.fori_loop(0, PIECES // 2, each, 0)
+        for index in range(4, 8):
+            legs[index - 4].wait_recv()
+            forward(index)
+        lax.fori_loop(PIECES // 2, PIECES, each, 0)
+        for copy in passes[4:]:
+            copy.wait_recv()
+        for copy in passes:
+            copy.wait_send()
+        for leg in legs:
+            leg.wait_send()
 
     loads[1].wait()
     loads[2].wait()
@@ -660,7 +695,7 @@
 
             @pl.when(high == 1)
             def _():
-                low_tile(step)
+                low_tile(step, 1)
 
             complete(step)
 
@@ -734,6 +769,7 @@
             dma((3,)), dma((18,)), dma((18,)), dma((2, 2)), dma((2, 3)), dma((2, 3)), dma((2, 3)), dma((2, 3)),
             dma((8,)), dma((8,)), dma((8,)), dma((8,)), dma((8,)), dma((8,)),
             dma((PIECES, N_Z)), dma((PIECES, N_Z)), dma((PIECES, N_Z)), dma((PIECES, N_Z)),
+            pltpu.VMEM((N_Z, 2, rows // 2, head), jnp.bfloat16), dma((4,)), dma((4,)),
         ],
         compiler_params=pltpu.CompilerParams(collective_id=3, has_side_effects=True, vmem_limit_bytes=VMEM_LIMIT),
         name="attention",

time: 161 us -> 159 us (0.988)
  Pallas kernels: 157 us -> 153 us
    pallas_call x1, Pallas kernels: 103 us -> 99.4 us  [attention(): pl.pallas_call(attention_kernel, out_shape=jax.ShapeDtypeStruct((rows, wi...]
where the time goes in v4:
time: 159 us; the launch traced here: 157 us
  Pallas kernels  153 us (96%)
  other arithmetic  2 us (1%)
  local copies, waits for them, and re-layouts  1.87 us (1%)
    pallas_call x1, Pallas kernels, attention(): pl.pallas_call(attention_kernel, out_shape=jax.ShapeDtypeStruct((rows, wi...  99.4 us
    pallas_call x1, Pallas kernels, hyena(): pl.pallas_call(hyena_kernel, out_shape=(jax.ShapeDtypeStruct((rows, chans...  53.8 us

profile of v4, /device:TPU:4, one launch (start us, length us, event | category | flops | bytes accessed | tf_op | source)
XLA Modules:
  0.0 157.2 jit_solution(8391489789549723170)
XLA Ops:
  0.0 1.0 fusion
  1.0 1.0 pad_maximum_fusion
  2.0 53.8 %hyena.1 = (bf16[512,512]{1,0:T(8,128)(2,1)}, bf16[512,2048]{1,0:T(8,128)(2,1)}) custom-call(bf16[3,512,512]{2,1,0:T(8,128)(2,1)} %bitcast.4, f32[3,7,32]{2,1,0:T(8,128)} %short_ref.1, f32[32,128]{1,0:T(8,128)} %bitcast.5, f32[1,512]{1,0:T(1,128)} %bitcast.7, bf16[512,512]{1,0:T(8,128)(2,1)} %base_ref.1, bf16[512,4096]{1,0:T(8,128)(2,1)} %first_weight.1, ...), custom_call_target="tpu_custom_call" | custom-call | tf_op jit(solution)/shard_map/hyena/pallas_call | solution.py:301
  55.9 99.4 %attention.1 = bf16[512,512]{1,0:T(8,128)(2,1)} custom-call(bf16[512,512]{1,0:T(8,128)(2,1)} %get-tuple-element.7.stream_ref, f32[1,4096]{1,0:T(1,128)} %bitcast.6, f32[512,128]{1,0:T(8,128)} %get-tuple-element.12.cos_ref, f32[512,128]{1,0:T(8,128)} %get-tuple-element.13.sin_ref, bf16[4096,1536]{1,0:T(8,128)(2,1)} %weight_ref.1, bf16[512,4096]{1,0:T(8,128)(2,1)} %own_ref.1, ...), custom_call_target="tpu_custom_call" | custom-call | tf_op jit(solution)/shard_map/attention/pallas_call | solution.py:748
  155.3 1.9 %copy.11 = bf16[512,512]{1,0:T(8,128)(2,1)} copy(bf16[512,512]{1,0:T(8,128)(2,1)} %attention.1) | data formatting | bytes 1048576
  (2 shorter events, 0.0 us)

commit v5 on v4

--- a/solution.py
+++ b/solution.py
@@ -364,7 +364,7 @@
     others = [lax.rem(z_pos + step, N_Z) for step in range(1, N_Z)]
     ring = [place(high, z, core) for z in others]
     diagonal = (((1 - high) * N_Z + z_pos) * 2 + core, (1 - x_lo) * N_Y + y_pos)
-    greet([dev_up, dev_down, partner, sibling, across, diagonal] + ring + [partner_place(z) for z in others])
+    greet([dev_up, dev_down, (ctx, x_lo * N_Y + opposite), partner, sibling, across, diagonal] + ring + [partner_place(z) for z in others])
 
     def slot(x, y):
         return x * N_Y + y
@@ -608,8 +608,9 @@
         return (ctx, x_lo * N_Y + lax.rem(y_pos + 1 + 2 * way, N_Y))
 
     def relay_copy(piece):
+        steps = 1 + 2 * lax.rem(piece, 2) - piece // (PIECES - 1)
         return remote(relay_out.at[piece], relay_in.at[piece], r_send.at[piece], r_recv.at[piece],
-                      way_place(lax.rem(piece, 2)))
+                      (ctx, x_lo * N_Y + lax.rem(y_pos + steps, N_Y)))
 
     def direct_copy(way, piece):
         return remote(outbox.at[way, piece], inbox.at[way, piece], y_send.at[way, piece], y_recv.at[way, piece],
@@ -633,7 +634,16 @@
         relay_copy(piece).start()
         outbox[1 - way, piece] = term(3 - 2 * way).astype(jnp.bfloat16)
         direct_copy(1 - way, piece).start()
-        pending[piece] = term(1 + 2 * way)
+
+        @pl.when(piece < PIECES - 1)
+        def _():
+            pending[piece] = term(1 + 2 * way)
+
+        @pl.when(piece == PIECES - 1)
+        def _():
+            outbox[way, piece] = term(1 + 2 * way).astype(jnp.bfloat16)
+            direct_copy(way, piece).start()
+
         kept[part, :] = term(0) + stream_ref[part, :].astype(jnp.float32)
 
     def combine(piece):
@@ -703,18 +713,24 @@
         def _():
             multiply(step - 1)
 
-        @pl.when(step >= 2)
+        @pl.when(jnp.logical_and(step >= 2, step <= PIECES))
         def _():
             combine(step - 2)
 
         return carry
 
-    lax.fori_loop(0, PIECES + 2, stage, 0)
+    lax.fori_loop(0, PIECES + 1, stage, 0)
 
     def finish(piece, carry):
         part = piece_at(piece)
         direct_copy(0, piece).wait_recv()
         direct_copy(1, piece).wait_recv()
+
+        @pl.when(piece == PIECES - 1)
+        def _():
+            relay_copy(piece).wait_recv()
+            kept[part, :] = kept[part, :] + relay_in[piece].astype(jnp.float32)
+
         total = kept[part, :] + inbox[0, piece].astype(jnp.float32) + inbox[1, piece].astype(jnp.float32)
         out_ref[part, :] = total.astype(jnp.bfloat16)
         return carry

time: 159 us -> 159 us (level); the launches traced: 157 us -> 159 us
  Pallas kernels: 153 us -> 155 us
    pallas_call x1, Pallas kernels: 99.4 us -> 101 us  [attention(): pl.pallas_call(attention_kernel, out_shape=jax.ShapeDtypeStruct((rows, wi...]
where the time goes in v5:
time: 159 us
  Pallas kernels  155 us (97%)
  other arithmetic  2 us (1%)
  local copies, waits for them, and re-layouts  1.87 us (1%)
    pallas_call x1, Pallas kernels, attention(): pl.pallas_call(attention_kernel, out_shape=jax.ShapeDtypeStruct((rows, wi...  101 us
    pallas_call x1, Pallas kernels, hyena(): pl.pallas_call(hyena_kernel, out_shape=(jax.ShapeDtypeStruct((rows, chans...  53.8 us

profile of v5, /device:TPU:4, one launch (start us, length us, event | category | flops | bytes accessed | tf_op | source)
XLA Modules:
  0.0 158.9 jit_solution(4730841774455706025)
XLA Ops:
  0.0 1.0 fusion
  1.0 1.0 pad_maximum_fusion
  2.0 53.8 %hyena.1 = (bf16[512,512]{1,0:T(8,128)(2,1)}, bf16[512,2048]{1,0:T(8,128)(2,1)}) custom-call(bf16[3,512,512]{2,1,0:T(8,128)(2,1)} %bitcast.4, f32[3,7,32]{2,1,0:T(8,128)} %short_ref.1, f32[32,128]{1,0:T(8,128)} %bitcast.5, f32[1,512]{1,0:T(1,128)} %bitcast.7, bf16[512,512]{1,0:T(8,128)(2,1)} %base_ref.1, bf16[512,4096]{1,0:T(8,128)(2,1)} %first_weight.1, ...), custom_call_target="tpu_custom_call" | custom-call | tf_op jit(solution)/shard_map/hyena/pallas_call | solution.py:301
  55.9 101.2 %attention.1 = bf16[512,512]{1,0:T(8,128)(2,1)} custom-call(bf16[512,512]{1,0:T(8,128)(2,1)} %get-tuple-element.7.stream_ref, f32[1,4096]{1,0:T(1,128)} %bitcast.6, f32[512,128]{1,0:T(8,128)} %get-tuple-element.12.cos_ref, f32[512,128]{1,0:T(8,128)} %get-tuple-element.13.sin_ref, bf16[4096,1536]{1,0:T(8,128)(2,1)} %weight_ref.1, bf16[512,4096]{1,0:T(8,128)(2,1)} %own_ref.1, ...), custom_call_target="tpu_custom_call" | custom-call | tf_op jit(solution)/shard_map/attention/pallas_call | solution.py:764
  157.1 1.9 %copy.11 = bf16[512,512]{1,0:T(8,128)(2,1)} copy(bf16[512,512]{1,0:T(8,128)(2,1)} %attention.1) | data formatting | bytes 1048576
  (2 shorter events, 0.0 us)
